TPU v7x, 128 devices: a whole 4x4x4 slice. The times are simulated.
128 devices in a mesh: areal: 16 (over x, y), layer: 8 (over z, core).
Axes of the slice: x: 4, y: 4, z: 4, core: 2. Of those that a mesh axis runs over, the one named last changes fastest.
Arguments:
- pressure: float32 [64, 4096, 256], P('layer', 'areal'), may hold values from -6 to 6
- saturations: float32 [2, 64, 4096, 256], P(None, 'layer', 'areal'), may hold values from 0.05 to 0.4
- old_saturations: float32 [2, 64, 4096, 256], P(None, 'layer', 'areal'), may hold values from 0.05 to 0.4
- permeability: float32 [64, 4096, 256], P('layer', 'areal'), may hold values from 0.05 to 5
- pore_volume: float32 [64, 4096, 256], P('layer', 'areal'), may hold values from 0.5 to 2
- perf_cell: int32 [8, 16, 16, 256], P('layer', 'areal'), may hold values from 0 to 65535
- perf_layer: int32 [8, 16, 16, 256], P('layer', 'areal'), may hold values from 0 to 7
- perf_seg: int32 [8, 16, 16, 256], P('layer', 'areal'), may hold values from 0 to 383
- perf_index: float32 [8, 16, 16, 256], P('layer', 'areal'), may hold values from 0.5 to 4
- perf_blocks: int32 [8, 16, 16], P('layer', 'areal'), may hold values from 0 to 2, as said below
- seg_parent: int32 [3072, 16], P('areal'), may hold values from 0 to 14, as said below
- seg_cond: float32 [3072, 16], P('areal'), may hold values from 10 to 100
- seg_target: float32 [3072, 16], P('areal'), may hold values from -6 to 6
Outputs:
- cell_residual: float32 [3, 64, 4096, 256], P(None, 'layer', 'areal')
- well_pressure: float32 [3072, 16], P('areal', 'layer')
Inputs may be any that keep to these rules, and one draw needn't show every extreme that they name: `perf_blocks`: in every layer one owner index, drawn from the seed, has 2 live blocks from every areal index. Apart from it, each owner has 2 live blocks from its own areal index, 1 to 2 from the areal indices next to it (circularly), and 0 to 1 from the others. `seg_parent`: segment 0 has parent 0; every other segment's parent is a lower segment of the same well.
All inputs are finite; a program needn't handle non-finite values.
Results may differ from a plain program's by a relative error of at most 0.0003.
Values sent between devices are 32-bit elements; how exact they have to be, the bound alone decides.
No kernel may reach another device: no remote copies, remote signals or barrier semaphores. Data moves between devices by JAX's collectives and lax.ppermute only.
A program may use at most 192 MiB of HBM per device.

v0:
```python
import functools

import jax
import jax.numpy as jnp
from jax import lax
from jax.experimental import pallas as pl
from jax.experimental.pallas import tpu as pltpu
from jax.sharding import PartitionSpec as P


CZ = 8
CX = 256
CY = 256
LANES = 128
ROWS = CZ * CX
WELLS_DEV = 192
SEG = 16
SEG_SLAB = 2
OWNERS = 16
ACCS = 4
N_LAYER = 8
DEVICES = OWNERS * N_LAYER
GROUP = WELLS_DEV // N_LAYER
HALF = 32
UNROLL = 4
VMEM_KERNEL = 26 << 20

MU_WATER = 0.5
MU_OIL = 2.0
MU_GAS = 0.2
GRAVITY = (0.35, 0.28, 0.07)
GEOMETRY = (0.4, 1.0, 1.0)
RELAX = 20.0

F32 = jnp.float32
I32 = jnp.int32


def mobilities(water, gas_sat):
    oil_sat = 1.0 - water - gas_sat
    return (
        water * water * (1.0 / MU_WATER),
        oil_sat * oil_sat * (1.0 / MU_OIL),
        gas_sat * gas_sat / MU_GAS,
    )


def in_hbm(value):
    return pltpu.with_memory_space_constraint(value, pltpu.HBM)


def iota(shape, dim):
    return lax.broadcasted_iota(I32, shape, dim)


def bcast_row(ref, row):
    return jnp.broadcast_to(ref[pl.ds(row, 1), :], (8, LANES))


def gather_kernel(
    blocks_s, p_hbm, sat_hbm, cell_ref, depth_ref, seg_ref, index_ref,
    sums_ref, rows_ref, ints_ref, floats_ref, p_rows, sat_rows, m_rows, p_groups, m_groups, rows_s, sem, sems
):
    to_smem = pltpu.make_async_copy(rows_ref, rows_s, sem)
    copies = []
    for z in range(CZ):
        for half in range(2):
            cols = pl.ds(half * LANES, LANES)
            at = pl.ds(half * ROWS + z * CX, CX)
            copies.append(
                [
                    pltpu.make_async_copy(
                        sat_hbm.at[0, z, :, cols], sat_rows.at[0, at, :], sems.at[z, half, 0]
                    ),
                    pltpu.make_async_copy(
                        sat_hbm.at[1, z, :, cols], sat_rows.at[1, at, :], sems.at[z, half, 1]
                    ),
                    pltpu.make_async_copy(
                        p_hbm.at[z, :, cols], p_rows.at[at, :], sems.at[z, half, 2]
                    ),
                ]
            )
            for copy in copies[-1]:
                copy.start()

    for half in range(2):
        cols = slice(half * LANES, (half + 1) * LANES)
        here = slice(half * OWNERS, (half + 1) * OWNERS)
        cell = cell_ref[0, 0, :, cols]
        seg = seg_ref[0, 0, :, cols]
        well = lax.shift_right_logical(seg, 1)
        group = lax.shift_right_logical(well * 2731, 16)
        rows_ref[here, :] = (
            (lax.shift_right_logical(cell, 7) & 1) * ROWS
            + depth_ref[0, 0, :, cols] * CX
            + lax.shift_right_logical(cell, 8)
        )
        ints_ref[0, here, :] = cell & (LANES - 1)
        ints_ref[1, here, :] = group
        ints_ref[2, here, :] = well - group * GROUP + (seg & 1) * HALF
        floats_ref[0, here, :] = index_ref[0, 0, :, cols]
    to_smem.start()

    for z in range(CZ):
        for half in range(2):
            for copy in copies[2 * z + half]:
                copy.wait()

            def dense(i, carry):
                at = pl.ds(pl.multiple_of(half * ROWS + z * CX + 64 * i, 64), 64)
                lam = mobilities(sat_rows[0, at, :], sat_rows[1, at, :])
                m_rows[at, :] = lam[0] + lam[1] + lam[2]
                return carry

            lax.fori_loop(0, CX // 64, dense, 0)

    to_smem.wait()
    sub = iota((8, LANES), 0)
    lane = iota((8, LANES), 1)
    places = iota((LANES, LANES), 0)

    def pick(owner, carry):
        for half in range(2):

            @pl.when(blocks_s[owner] > half)
            def _():
                block = half * OWNERS + owner
                for group in range(16):
                    grp_p = None
                    grp_m = None
                    for i in range(8):
                        row = rows_s[block, 8 * group + i]
                        row_p = jnp.broadcast_to(p_rows[pl.ds(row, 1), :], (8, LANES))
                        row_m = jnp.broadcast_to(m_rows[pl.ds(row, 1), :], (8, LANES))
                        grp_p = row_p if i == 0 else jnp.where(sub == i, row_p, grp_p)
                        grp_m = row_m if i == 0 else jnp.where(sub == i, row_m, grp_m)
                    p_groups[block, 8 * group : 8 * group + 8, :] = grp_p
                    m_groups[block, 8 * group : 8 * group + 8, :] = grp_m

        return carry

    lax.fori_loop(0, OWNERS, pick, 0)

    def reduce(step, carry):
        for unit in range(UNROLL):
            owner = step * UNROLL + unit
            count = blocks_s[owner]
            values = []
            hots = []
            for half in range(2):
                block = half * OWNERS + owner
                lane_of = jnp.broadcast_to(ints_ref[0, pl.ds(block, 1), :], (8, LANES))
                acc_p = jnp.zeros((8, LANES), F32)
                acc_m = jnp.zeros((8, LANES), F32)
                for group in range(16):
                    keep = lane == 8 * group + sub
                    at = slice(8 * group, 8 * group + 8)
                    grp_p = jnp.take_along_axis(p_groups[block, at, :], lane_of, axis=1)
                    grp_m = jnp.take_along_axis(m_groups[block, at, :], lane_of, axis=1)
                    acc_p = jnp.where(keep, grp_p, acc_p)
                    acc_m = jnp.where(keep, grp_m, acc_m)
                live = count > half
                press = jnp.where(live, jnp.sum(acc_p, axis=0, keepdims=True), 0.0)
                total = jnp.where(live, jnp.sum(acc_m, axis=0, keepdims=True), 0.0)
                floats_ref[1, pl.ds(block, 1), :] = press
                mobile = floats_ref[0, pl.ds(block, 1), :] * total
                group_of = jnp.broadcast_to(ints_ref[1, pl.ds(block, 1), :], (8, LANES)) == sub
                for v in (mobile, mobile * press):
                    values.append(jnp.where(group_of, jnp.broadcast_to(v, (8, LANES)), 0.0))
                spot = jnp.broadcast_to(ints_ref[2, pl.ds(block, 1), :], (LANES, LANES))
                hots += [spot == places, spot == places - 2 * HALF]
            value = jnp.concatenate(values, axis=1)
            high = value.astype(jnp.bfloat16).astype(F32)
            rest = value - high
            middle = rest.astype(jnp.bfloat16).astype(F32)
            low = rest - middle
            pieces = jnp.concatenate([high, middle, low], axis=0).astype(jnp.bfloat16)
            hot = jnp.concatenate(hots, axis=1).astype(F32).astype(jnp.bfloat16)
            out = lax.dot_general(
                pieces, hot, (((1,), (1,)), ((), ())), preferred_element_type=F32
            )
            panel = pl.ds(pl.multiple_of(owner * N_LAYER, 8), N_LAYER)
            sums_ref[panel, :] = out[0:8] + out[8:16] + out[16:24]
        return carry

    lax.fori_loop(0, OWNERS // UNROLL, reduce, 0)


def gather_sums(blocks, pressure, saturations, cell, depth, seg, index):
    hbm = pl.BlockSpec(memory_space=pl.ANY)
    vmem = pl.BlockSpec(memory_space=pltpu.VMEM)
    return pl.pallas_call(
        gather_kernel,
        in_specs=[pl.BlockSpec(memory_space=pltpu.SMEM), hbm, hbm] + [vmem] * 4,
        out_specs=[vmem] * 4,
        out_shape=[
            jax.ShapeDtypeStruct((DEVICES, LANES), F32),
            jax.ShapeDtypeStruct((2 * OWNERS, LANES), I32),
            jax.ShapeDtypeStruct((3, 2 * OWNERS, LANES), I32),
            jax.ShapeDtypeStruct((2, 2 * OWNERS, LANES), F32),
        ],
        scratch_shapes=[
            pltpu.VMEM((2 * ROWS, LANES), F32),
            pltpu.VMEM((2, 2 * ROWS, LANES), F32),
            pltpu.VMEM((2 * ROWS, LANES), F32),
            pltpu.VMEM((2 * OWNERS, LANES, LANES), F32),
            pltpu.VMEM((2 * OWNERS, LANES, LANES), F32),
            pltpu.SMEM((2 * OWNERS, LANES), I32),
            pltpu.SemaphoreType.DMA(()),
            pltpu.SemaphoreType.DMA((CZ, 2, 3)),
        ],
        compiler_params=pltpu.CompilerParams(vmem_limit_bytes=VMEM_KERNEL),
        cost_estimate=pl.CostEstimate(flops=0, bytes_accessed=24 << 20, transcendentals=0),
        name="gather_sums",
    )(blocks, in_hbm(pressure), in_hbm(saturations), cell, depth, seg, index)


def pack_kernel(
    parity_s, p_hbm, sat_hbm, k_hbm, plane_even_ref, plane_odd_ref, row_even_ref, row_odd_ref, edges, sems
):
    z_odd, x_odd = parity_s[0], parity_s[1]
    sources = (p_hbm, sat_hbm.at[0], sat_hbm.at[1], k_hbm)
    planes, sides = [], []
    for f, source in enumerate(sources):
        first = (1 - z_odd) * (CZ - 1)
        planes.append(
            pltpu.make_async_copy(source.at[first], plane_even_ref.at[f], sems.at[0, f])
        )
        planes.append(
            pltpu.make_async_copy(source.at[CZ - 1 - first], plane_odd_ref.at[f], sems.at[1, f])
        )
        for side, row in ((0, CX - 8), (1, 0)):
            sides.append(
                pltpu.make_async_copy(
                    source.at[:, pl.ds(row, 8), :], edges.at[side, f], sems.at[2 + side, f]
                )
            )
    for copy in sides + planes:
        copy.start()
    for copy in sides:
        copy.wait()
    swap = x_odd == 1
    for f in range(4):
        for z in range(CZ):
            last = edges[0, f, z, 7:8, :]
            first = edges[1, f, z, 0:1, :]
            row_even_ref[f, z : z + 1, :] = jnp.where(swap, first, last)
            row_odd_ref[f, z : z + 1, :] = jnp.where(swap, last, first)
    for copy in planes:
        copy.wait()


def pack_halos(parity, pressure, saturations, permeability):
    hbm = pl.BlockSpec(memory_space=pl.ANY)
    vmem = pl.BlockSpec(memory_space=pltpu.VMEM)
    return pl.pallas_call(
        pack_kernel,
        in_specs=[pl.BlockSpec(memory_space=pltpu.SMEM)] + [hbm] * 3,
        out_specs=[vmem] * 4,
        out_shape=[
            jax.ShapeDtypeStruct((4, CX, CY), F32),
            jax.ShapeDtypeStruct((4, CX, CY), F32),
            jax.ShapeDtypeStruct((4, CZ, CY), F32),
            jax.ShapeDtypeStruct((4, CZ, CY), F32),
        ],
        scratch_shapes=[
            pltpu.VMEM((2, 4, CZ, 8, CY), F32),
            pltpu.SemaphoreType.DMA((4, 4)),
        ],
        compiler_params=pltpu.CompilerParams(vmem_limit_bytes=VMEM_KERNEL),
        cost_estimate=pl.CostEstimate(flops=0, bytes_accessed=6 << 20, transcendentals=0),
        name="pack_halos",
    )(parity, in_hbm(pressure), in_hbm(saturations), in_hbm(permeability))


def solve_kernel(sums_ref, parent_ref, cond_ref, target_ref, send_ref, parts):
    total = sums_ref[0:N_LAYER, :]
    for owner in range(1, OWNERS):
        total = total + sums_ref[owner * N_LAYER : (owner + 1) * N_LAYER, :]
    for part in range(4):
        parts[part] = pltpu.roll(total, LANES - HALF * part, 1) if part else total

    ground, load, parent, cond = [], [], [], []
    for s in range(SEG):
        z, k = divmod(s, SEG_SLAB)
        ground.append(parts[k, z : z + 1, :] + RELAX)
        load.append(parts[2 + k, z : z + 1, :] + RELAX * target_ref[s : s + 1, :])
        parent.append(parent_ref[s : s + 1, :])
        cond.append(cond_ref[s : s + 1, :])
    share, own = [None] * SEG, [None] * SEG
    for s in range(SEG - 1, 0, -1):
        inverse = 1.0 / (ground[s] + cond[s])
        share[s] = cond[s] * inverse
        own[s] = load[s] * inverse
        add_ground = share[s] * ground[s]
        add_load = share[s] * load[s]
        for j in range(s):
            hit = parent[s] == j
            ground[j] = ground[j] + jnp.where(hit, add_ground, 0.0)
            load[j] = load[j] + jnp.where(hit, add_load, 0.0)
    value = [load[0] / ground[0]]
    for s in range(1, SEG):
        above = value[0]
        for j in range(1, s):
            above = jnp.where(parent[s] == j, value[j], above)
        value.append(own[s] + share[s] * above)
    for s in range(SEG):
        z, k = divmod(s, SEG_SLAB)
        parts[k, z : z + 1, :] = value[s]
    first = iota((N_LAYER, LANES), 1) < HALF
    panel = jnp.where(first, parts[0], pltpu.roll(parts[1], HALF, 1))
    for owner in range(OWNERS):
        send_ref[owner * N_LAYER : (owner + 1) * N_LAYER, :] = panel


def solve_wells(sums, parent, cond, target):
    vmem = pl.BlockSpec(memory_space=pltpu.VMEM)
    return pl.pallas_call(
        solve_kernel,
        in_specs=[vmem] * 4,
        out_specs=vmem,
        out_shape=jax.ShapeDtypeStruct((DEVICES, LANES), F32),
        scratch_shapes=[pltpu.VMEM((4, N_LAYER, LANES), F32)],
        compiler_params=pltpu.CompilerParams(vmem_limit_bytes=4 << 20),
        cost_estimate=pl.CostEstimate(flops=0, bytes_accessed=1 << 20, transcendentals=0),
        name="solve_wells",
    )(sums, parent, cond, target)


def doubled_mobilities(water, gas_sat):
    oil_sat = 1.0 - water - gas_sat
    return (
        water * water * (2.0 / MU_WATER),
        oil_sat * oil_sat * (2.0 / MU_OIL),
        gas_sat * gas_sat * (2.0 / MU_GAS),
    )


def half_harmonic(left, right):
    return left * right / (left + right)


STRIP = 32


def wide(ref, *index):
    *lead, start, size = index
    return jnp.concatenate(
        [ref[(*lead, pl.ds(half * ROWS + start, size), slice(None))] for half in range(2)], axis=1
    )


def flow_kernel(
    z0, nz, parity_s, p_hbm, sat_hbm, k_hbm, plane_even_ref, plane_odd_ref, row_even_ref, row_odd_ref,
    old_ref, pore_ref, out_ref,
    cells, lams, rolled, zflux, sems
):
    step_at = pl.program_id(0)
    layer = step_at + z0
    now = lax.rem(step_at, 2)
    later = 1 - now
    halo_below = z0 == 0
    first_plane = z0 if halo_below else z0 - 1
    last_plane = z0 + nz if halo_below else z0 + nz - 1

    def plane_copies(z):
        sources = (p_hbm.at[z], sat_hbm.at[0, z], sat_hbm.at[1, z], k_hbm.at[z])
        return [
            pltpu.make_async_copy(source, cells.at[f, z], sems.at[z, f])
            for f, source in enumerate(sources)
        ]

    def vertical(low, high):
        trans = GEOMETRY[0] * half_harmonic(low[1], high[1])
        drop = low[0] - high[0]
        flux = []
        for a in range(3):
            potential = drop + GRAVITY[a]
            flux.append(trans * potential * jnp.where(potential > 0, low[2 + a], high[2 + a]))
        return flux

    def level(low, high, mask=None):
        drop = low[0] - high[0]
        rate = half_harmonic(low[1], high[1]) * drop
        if mask is not None:
            rate = jnp.where(mask, 0.0, rate)
        return [rate * jnp.where(drop > 0, low[2 + a], high[2 + a]) for a in range(3)]

    def cell_at(z, row, size):
        rows = pl.ds(row, size)
        return (
            [cells[0, z, rows, :], cells[3, z, rows, :]],
            [cells[1, z, rows, :], cells[2, z, rows, :]],
        )

    halo_from_even = parity_s[0] == (1 if halo_below else 0)

    def halo_at(row, size):
        rows = pl.ds(row, size)
        value = [
            jnp.where(halo_from_even, plane_even_ref[f, rows, :], plane_odd_ref[f, rows, :])
            for f in range(4)
        ]
        return [value[0], value[3]], [value[1], value[2]]

    def here_at(row, size):
        rows = pl.ds(row, size)
        return [cells[0, layer, rows, :], cells[3, layer, rows, :]] + [
            lams[now, a, rows, :] for a in range(3)
        ]

    @pl.when(step_at == 0)
    def _():
        for z in range(first_plane, last_plane + 1):
            for copy in plane_copies(z):
                copy.start()
        for z in range(first_plane, z0 + 1):
            for copy in plane_copies(z):
                copy.wait()

        def first(i, carry):
            row = pl.multiple_of(STRIP * i, STRIP)
            low, low_sat = halo_at(row, STRIP) if halo_below else cell_at(z0 - 1, row, STRIP)
            high, high_sat = cell_at(z0, row, STRIP)
            lam = doubled_mobilities(*high_sat)
            flux = vertical(low + list(doubled_mobilities(*low_sat)), high + list(lam))
            for a in range(3):
                lams[0, a, pl.ds(row, STRIP), :] = lam[a]
                zflux[a, pl.ds(row, STRIP), :] = flux[a]
            return carry

        lax.fori_loop(0, CX // STRIP, first, 0)

    sub = iota((STRIP, CY), 0)
    top = iota((8, CY), 0) == 0
    last_lane = iota((STRIP, CY), 1) == CY - 1

    def side_row(from_even):
        here = pl.ds(layer, 1)
        value = [
            jnp.where(from_even, row_even_ref[f, here, :], row_odd_ref[f, here, :])
            for f in range(4)
        ]
        return [value[0], value[3]] + list(doubled_mobilities(value[1], value[2]))

    east = side_row(parity_s[1] == 0)
    flux = level(side_row(parity_s[1] == 1), [v[0:1] for v in here_at(0, 8)])
    down = tuple(jnp.broadcast_to(f, (8, CY)) for f in flux)
    for f, value in enumerate(here_at(0, STRIP)):
        rolled[f] = pltpu.roll(value, CY - 1, 1)

    def sweep(next_at):
        def step(i, carry):
            row = pl.multiple_of(STRIP * i, STRIP)
            at = pl.ds(row, STRIP)
            final = i == CX // STRIP - 1
            here = here_at(row, STRIP)
            flux_y = level(here, [rolled[f] for f in range(5)], last_lane)
            back_y = [pltpu.roll(f, 1, 1) for f in flux_y]
            after = here_at(
                pl.multiple_of(jnp.minimum(row + STRIP, CX - STRIP), STRIP), STRIP
            )
            after_rolled = [pltpu.roll(v, CY - 1, 1) for v in after]
            neighbour = [
                jnp.where(
                    sub == STRIP - 1,
                    jnp.broadcast_to(jnp.where(final, e, n[0:1]), (STRIP, CY)),
                    pltpu.roll(v, STRIP - 1, 0),
                )
                for v, n, e in zip(here, after, east)
            ]
            flux_x = level(here, neighbour)
            down_x = [pltpu.roll(f, 1, 0) for f in flux_x]
            heads = tuple(d[0:8] for d in down_x)
            high, high_sat = next_at(row, STRIP)
            lam = doubled_mobilities(*high_sat)
            flux_z = vertical(here, high + list(lam))
            water = cells[1, layer, at, :]
            gas = cells[2, layer, at, :]
            old_water = old_ref[0, 0, at, :]
            old_gas = old_ref[1, 0, at, :]
            pore = pore_ref[0, at, :]
            change = [
                water - old_water,
                (1.0 - water - gas) - (1.0 - old_water - old_gas),
                gas - old_gas,
            ]
            for a in range(3):
                lams[later, a, at, :] = lam[a]
                net = flux_z[a] - zflux[a, at, :]
                zflux[a, at, :] = flux_z[a]
                before = jnp.concatenate(
                    [jnp.where(top, carry[a], heads[a]), down_x[a][8:]], axis=0
                )
                net = net + (flux_x[a] - before)
                net = net + (flux_y[a] - back_y[a])
                out_ref[a, 0, at, :] = pore * change[a] + net
            for f in range(5):
                rolled[f] = after_rolled[f]
            return heads

        lax.fori_loop(0, CX // STRIP, step, down)

    inside = nz if halo_below else nz - 1

    @pl.when(step_at < inside)
    def _():
        for copy in plane_copies(layer + 1):
            copy.wait()
        sweep(lambda row, size: cell_at(layer + 1, row, size))

    if not halo_below:

        @pl.when(step_at == inside)
        def _():
            sweep(halo_at)


def cell_flows(z0, nz, parity, pressure, saturations, permeability, planes, sides, old, pore):
    hbm = pl.BlockSpec(memory_space=pl.ANY)
    vmem = pl.BlockSpec(memory_space=pltpu.VMEM)
    return pl.pallas_call(
        functools.partial(flow_kernel, z0, nz),
        grid=(nz,),
        in_specs=[pl.BlockSpec(memory_space=pltpu.SMEM), hbm, hbm, hbm, vmem, vmem, vmem, vmem]
        + [
            pl.BlockSpec((2, 1, CX, CY), lambda z: (0, z + z0, 0, 0)),
            pl.BlockSpec((1, CX, CY), lambda z: (z + z0, 0, 0)),
        ],
        out_specs=pl.BlockSpec((3, 1, CX, CY), lambda z: (0, z, 0, 0)),
        out_shape=pltpu.HBM((3, nz, CX, CY), F32),
        scratch_shapes=[
            pltpu.VMEM((4, CZ, CX, CY), F32),
            pltpu.VMEM((2, 3, CX, CY), F32),
            pltpu.VMEM((5, STRIP, CY), F32),
            pltpu.VMEM((3, CX, CY), F32),
            pltpu.SemaphoreType.DMA((CZ, 4)),
        ],
        compiler_params=pltpu.CompilerParams(vmem_limit_bytes=VMEM_KERNEL),
        cost_estimate=pl.CostEstimate(flops=0, bytes_accessed=20 << 20, transcendentals=0),
    )(
        parity, in_hbm(pressure), in_hbm(saturations), in_hbm(permeability), *planes, *sides, in_hbm(old), in_hbm(pore)
    )


def inflow_kernel(
    rows_s, blocks_s, areal_s, pw_ref, ints_ref, floats_ref, low_hbm, high_hbm, sat_hbm,
    out_ref, slab_ref, rate, flows, sats, sems, *sums
):
    layer = pl.program_id(0)

    def layer_copies(source, at, z):
        return [
            pltpu.make_async_copy(source.at[a, at], flows.at[a, z], sems.at[z, a]) for a in range(3)
        ] + [
            pltpu.make_async_copy(sat_hbm.at[a, z], sats.at[a, z], sems.at[z, 3 + a]) for a in range(2)
        ]

    @pl.when(layer == 0)
    def _():
        for z in range(CZ):
            source = low_hbm if z < CZ // 2 else high_hbm
            for copy in layer_copies(source, z % (CZ // 2), z):
                copy.start()
        zero = jnp.zeros((64, LANES), F32)

        def clear(i, carry):
            for acc in sums:
                acc[pl.ds(pl.multiple_of(64 * i, 64), 64), :] = zero
            return carry

        lax.fori_loop(0, 2 * ROWS // 64, clear, 0)
        panels = [pw_ref[pl.ds(g, OWNERS, stride=N_LAYER), :] for g in range(N_LAYER)]
        for half in range(2):
            here = slice(half * OWNERS, (half + 1) * OWNERS)
            group = ints_ref[1, here, :]
            spot = ints_ref[2, here, :]
            well_press = jnp.take_along_axis(panels[0], spot, axis=1)
            for g in range(1, N_LAYER):
                well_press = jnp.where(
                    group == g, jnp.take_along_axis(panels[g], spot, axis=1), well_press
                )
            rate[here, :] = floats_ref[0, here, :] * (floats_ref[1, here, :] - well_press)

        sub = iota((8, LANES), 0)
        lane = iota((8, LANES), 1)

        mine = pw_ref[pl.ds(pl.multiple_of(areal_s[0] * N_LAYER, 8), N_LAYER), :]
        for tile in range(2):
            well = lane + tile * LANES
            group = lax.shift_right_logical(well * 2731, 16)
            for k in range(SEG_SLAB):
                spot = jnp.minimum(well - group * GROUP + k * HALF, LANES - 1)
                value = jnp.where(group == sub, jnp.take_along_axis(mine, spot, axis=1), 0.0)
                value = jnp.sum(value, axis=0, keepdims=True)
                width = min(LANES, WELLS_DEV - tile * LANES)
                slab_ref[k : k + 1, tile * LANES : tile * LANES + width] = value[:, :width]

        def owner_step(owner, carry):
            count = blocks_s[owner]
            for half in range(2):

                @pl.when(count > half)
                def _():
                    block = half * OWNERS + owner
                    lane_of = jnp.broadcast_to(ints_ref[0, pl.ds(block, 1), :], (8, LANES))
                    rate_of = bcast_row(rate, block)
                    for group in range(16):
                        pick = sub + 8 * group
                        place = jnp.take_along_axis(lane_of, pick, axis=1)
                        value = jnp.take_along_axis(rate_of, pick, axis=1)
                        value = jnp.where(lane == place, value, 0.0)
                        for i in range(8):
                            row = rows_s[block, 8 * group + i]
                            acc = sums[i % ACCS]
                            acc[pl.ds(row, 1), :] += value[i : i + 1, :]

            return carry

        lax.fori_loop(0, OWNERS, owner_step, 0)

    for copy in layer_copies(low_hbm, 0, layer):
        copy.wait()

    def combine(i, carry):
        row = pl.multiple_of(32 * i, 32)
        here = pl.ds(row, 32)
        base = pl.multiple_of(layer * CX + row, 8)
        lam = mobilities(sats[0, layer, here, :], sats[1, layer, here, :])
        total = wide(sums[0], base, 32)
        for acc in sums[1:]:
            total = total + wide(acc, base, 32)
        for a in range(3):
            out_ref[a, 0, here, :] = flows[a, layer, here, :] + lam[a] * total
        return carry

    lax.fori_loop(0, CX // 32, combine, 0)


def add_inflow(rows, blocks, areal, pw, ints, floats, low, high, saturations):
    hbm = pl.BlockSpec(memory_space=pl.ANY)
    flow_spec = pl.BlockSpec((3, 1, CX, CY), lambda z, *_: (0, z, 0, 0))
    return pl.pallas_call(
        inflow_kernel,
        grid_spec=pltpu.PrefetchScalarGridSpec(
            num_scalar_prefetch=3,
            grid=(CZ,),
            in_specs=[
                pl.BlockSpec((DEVICES, LANES), lambda z, *_: (0, 0)),
                pl.BlockSpec((3, 2 * OWNERS, LANES), lambda z, *_: (0, 0, 0)),
                pl.BlockSpec((2, 2 * OWNERS, LANES), lambda z, *_: (0, 0, 0)),
                hbm,
                hbm,
                hbm,
            ],
            out_specs=[flow_spec, pl.BlockSpec((SEG_SLAB, WELLS_DEV), lambda z, *_: (0, 0))],
            scratch_shapes=[
                pltpu.VMEM((2 * OWNERS, LANES), F32),
                pltpu.VMEM((3, CZ, CX, CY), F32),
                pltpu.VMEM((2, CZ, CX, CY), F32),
                pltpu.SemaphoreType.DMA((CZ, 5)),
            ]
            + [pltpu.VMEM((2 * ROWS, LANES), F32) for _ in range(ACCS)],
        ),
        out_shape=[
            jax.ShapeDtypeStruct((3, CZ, CX, CY), F32),
            jax.ShapeDtypeStruct((SEG_SLAB, WELLS_DEV), F32),
        ],
        compiler_params=pltpu.CompilerParams(vmem_limit_bytes=VMEM_KERNEL),
        cost_estimate=pl.CostEstimate(flops=0, bytes_accessed=24 << 20, transcendentals=0),
        name="add_inflow",
    )(rows, blocks, areal, pw, ints, floats, in_hbm(low), in_hbm(high), in_hbm(saturations))


def on_device(
    pressure,
    saturations,
    old_saturations,
    permeability,
    pore_volume,
    perf_cell,
    perf_layer,
    perf_seg,
    perf_index,
    perf_blocks,
    seg_parent,
    seg_cond,
    seg_target,
):
    n_areal = lax.axis_size("areal")
    n_layer = lax.axis_size("layer")
    layer = lax.axis_index("layer").astype(I32)
    areal = lax.axis_index("areal").astype(I32).reshape(1)
    blocks = perf_blocks[0, 0]
    depth = CZ // 2
    parity = jnp.concatenate([layer.reshape(1), areal]) & 1

    def own_wells(values):
        part = lax.dynamic_slice_in_dim(values, layer * GROUP, GROUP, axis=0)
        return jnp.pad(part.T, ((0, 0), (0, LANES - GROUP)))

    def flows(z0):
        return cell_flows(
            z0, depth, parity, pressure, saturations, permeability, planes, sides, old_saturations, pore_volume
        )

    def even_swap(values, axis, count):
        return lax.ppermute(values, axis, [(i, i ^ 1) for i in range(count)])

    def odd_swap(values, axis, count):
        pairs = [(i, i + 1) for i in range(1, count - 1, 2)]
        return lax.ppermute(values, axis, pairs + [(j, i) for i, j in pairs])

    def exchange(values):
        return lax.all_to_all(values, ("areal", "layer"), split_axis=0, concat_axis=0, tiled=True)

    packed = pack_halos(parity, pressure, saturations, permeability)
    plane_even = even_swap(packed[0], "layer", n_layer)
    plane_odd = odd_swap(packed[1], "layer", n_layer)
    row_even = even_swap(packed[2], "areal", n_areal)
    row_odd = odd_swap(packed[3], "areal", n_areal)
    planes, sides = (plane_even, plane_odd), (row_even, row_odd)
    sums, rows, ints, floats = gather_sums(
        blocks, pressure, saturations, perf_cell, perf_layer, perf_seg, perf_index
    )
    received = exchange(sums)
    low = flows(0)
    systems = [own_wells(v) for v in (seg_parent, seg_cond, seg_target)]
    solved = solve_wells(received, *systems)
    pw = exchange(solved)
    high = flows(depth)
    residual, slab = add_inflow(rows, blocks, areal, pw, ints, floats, low, high, saturations)
    return residual, slab.T


def solution(mesh):
    return jax.shard_map(
        on_device,
        mesh=mesh,
        in_specs=(
            P("layer", "areal", None),
            P(None, "layer", "areal", None),
            P(None, "layer", "areal", None),
            P("layer", "areal", None),
            P("layer", "areal", None),
            P("layer", "areal", None, None),
            P("layer", "areal", None, None),
            P("layer", "areal", None, None),
            P("layer", "areal", None, None),
            P("layer", "areal", None),
            P("areal", None),
            P("areal", None),
            P("areal", None),
        ),
        out_specs=(P(None, "layer", "areal", None), P("areal", "layer")),
        check_vma=False,
    )
```

profile of v0, /device:TPU:4, one launch (start us, length us, event | category | flops | bytes accessed | tf_op | source)
XLA Modules:
  0.0 82.1 jit_solution(3426299760268378751)
XLA Ops:
  0.6 0.0 copy-start
  0.6 0.1 add_and_fusion.parity_s
  0.7 0.0 copy-start.5
  0.7 3.4 %pack_halos.1 = (f32[4,256,256]{2,1,0:T(8,128)}, f32[4,256,256]{2,1,0:T(8,128)S(1)}, f32[4,8,256]{2,1,0:T(8,128)S(1)}, f32[4,8,256]{2,1,0:T(8,128)S(1)}) custom-call(s32[2]{0:T(128)S(1)} %add_and_fusion.parity_s, f32[8,256,256]{2,1,0:T(8,128)} %p_hbm.7, f32[2,8,256,256]{3,2,1,0:T(8,128)} %sat_hbm.9, f32[8,256,256]{2,1,0:T(8,128)} %k_hbm.5), custom_call_target="tpu_custom_call" | custom-call | bytes 6291456 | tf_op jit(solution)/shard_map/pack_halos/pallas_call | solution.py:256
  4.2 0.1 collective-permute-start
  4.3 0.7 collective-permute-start.1
  5.1 0.0 copy-start.6
  5.1 0.0 copy-start.7
  5.1 9.4 %gather_sums.1 = (f32[128,128]{1,0:T(8,128)}, s32[32,128]{1,0:T(8,128)S(1)}, s32[3,32,128]{2,1,0:T(8,128)S(1)}, f32[2,32,128]{2,1,0:T(8,128)S(1)}) custom-call(s32[16]{0:T(128)S(1)} %bitcast.20, f32[8,256,256]{2,1,0:T(8,128)} %p_hbm.7, f32[2,8,256,256]{3,2,1,0:T(8,128)} %sat_hbm.9, s32[1,1,16,256]{3,2,1,0:T(8,128)S(1)} %copy-done.1, ...), custom_call_target="tpu_custom_call" | custom-call | bytes 25165824 | tf_op jit(solution)/shard_map/gather_sums/pallas_call | solution.py:192
  14.5 12.4 %all-to-all-start = ((f32[128,1,128]{2,1,0:T(1,128)}), f32[128,1,128]{2,1,0:T(1,128)S(1)}, u32[]{:S(2)}, u32[]{:S(2)}) async-start(f32[128,1,128]{2,1,0:T(1,128)} %bitcast.3), calls=%async_computation | async-start | bytes 131072 | tf_op jit(solution)/shard_map/all_to_all | solution.py:715
  26.9 0.1 dynamic-slice_bitcast_fusion.2
  27.0 0.1 dynamic-slice_bitcast_fusion
  27.1 7.8 %all-to-all-done = f32[128,1,128]{2,1,0:T(1,128)S(1)} async-done(((f32[128,1,128]{2,1,0:T(1,128)}), f32[128,1,128]{2,1,0:T(1,128)S(1)}, u32[]{:S(2)}, u32[]{:S(2)}) %all-to-all-start) | async-done | bytes 65568 | tf_op jit(solution)/shard_map/all_to_all | solution.py:715
  34.9 1.0 %solve_wells.1 = f32[128,128]{1,0:T(8,128)} custom-call(f32[128,128]{1,0:T(8,128)S(1)} %bitcast.19, s32[16,128]{1,0:T(8,128)S(1)} %pad.11.parent_ref, f32[16,128]{1,0:T(8,128)S(1)} %pad.12.cond_ref, f32[16,128]{1,0:T(8,128)S(1)} %pad.13.target_ref), custom_call_target="tpu_custom_call" | custom-call | bytes 1048576 | tf_op jit(solution)/shard_map/solve_wells/pallas_call | solution.py:318
  35.9 6.2 %all-to-all-start.1 = ((f32[128,1,128]{2,1,0:T(1,128)}), f32[128,1,128]{2,1,0:T(1,128)S(1)}, u32[]{:S(2)}, u32[]{:S(2)}) async-start(f32[128,1,128]{2,1,0:T(1,128)} %bitcast.9), calls=%async_computation.1 | async-start | bytes 131072 | tf_op jit(solution)/shard_map/all_to_all | solution.py:715
  42.1 1.5 %collective-permute-start.2 = (f32[4,8,256]{2,1,0:T(8,128)S(1)}, f32[4,8,256]{2,1,0:T(8,128)S(1)}, u32[]{:S(2)}, u32[]{:S(2)}) collective-permute-start(f32[4,8,256]{2,1,0:T(8,128)S(1)} %get-tuple-element.18), channel_id=1, source_target_pairs={{0,8},{8,0},{16,24},{24,16},{32,40},{40,32},{48,56},{56,48},{64,72... | collective-permute-start | bytes 98312 | tf_op jit(solution)/shard_map/ppermute | solution.py:708
  43.7 4.0 %collective-permute-start.3 = (f32[4,8,256]{2,1,0:T(8,128)S(1)}, f32[4,8,256]{2,1,0:T(8,128)S(1)}, u32[]{:S(2)}, u32[]{:S(2)}) collective-permute-start(f32[4,8,256]{2,1,0:T(8,128)S(1)} %get-tuple-element.19), channel_id=1, source_target_pairs={{8,16},{24,32},{40,48},{56,64},{72,80},{88,96},{104,112},{16,8},{3... | collective-permute-start | bytes 98312 | tf_op jit(solution)/shard_map/ppermute | solution.py:712
  47.6 0.0 collective-permute-done.2.row_even_ref
  47.6 3.9 %collective-permute-done.3.row_odd_ref = f32[4,8,256]{2,1,0:T(8,128)S(1)} collective-permute-done((f32[4,8,256]{2,1,0:T(8,128)S(1)}, f32[4,8,256]{2,1,0:T(8,128)S(1)}, u32[]{:S(2)}, u32[]{:S(2)}) %collective-permute-start.3) | collective-permute-done | bytes 32800 | tf_op jit(solution)/shard_map/ppermute | solution.py:712
  51.6 0.0 collective-permute-done.plane_even_ref
  51.6 0.0 collective-permute-done.1.plane_odd_ref
  51.6 10.0 %shard_map.141.high_hbm = f32[3,4,256,256]{3,2,1,0:T(8,128)} custom-call(s32[2]{0:T(128)S(1)} %add_and_fusion.parity_s, f32[8,256,256]{2,1,0:T(8,128)} %p_hbm.7, f32[2,8,256,256]{3,2,1,0:T(8,128)} %sat_hbm.9, f32[8,256,256]{2,1,0:T(8,128)} %k_hbm.5, f32[4,256,256]{2,1,0:T(8,128)S(1)} %collective-permute-done.plane_even_ref, ...), custom_call_target="tpu_custom_call" | custom-call | bytes 20971520 | tf_op jit(solution)/shard_map/pallas_call | solution.py:522
  61.6 9.8 %shard_map.140.low_hbm = f32[3,4,256,256]{3,2,1,0:T(8,128)} custom-call(s32[2]{0:T(128)S(1)} %add_and_fusion.parity_s, f32[8,256,256]{2,1,0:T(8,128)} %p_hbm.7, f32[2,8,256,256]{3,2,1,0:T(8,128)} %sat_hbm.9, f32[8,256,256]{2,1,0:T(8,128)} %k_hbm.5, f32[4,256,256]{2,1,0:T(8,128)S(1)} %collective-permute-done.plane_even_ref, ...), custom_call_target="tpu_custom_call" | custom-call | bytes 20971520 | tf_op jit(solution)/shard_map/pallas_call | solution.py:522
  71.5 10.6 %add_inflow.1 = (f32[3,8,256,256]{3,2,1,0:T(8,128)}, f32[2,192]{1,0:T(2,128)}) custom-call(s32[32,128]{1,0:T(8,128)S(1)} %get-tuple-element.12.rows_s, s32[16]{0:T(128)S(1)} %bitcast.21, s32[1]{0:T(128)} %bitcast.1.areal_s, f32[128,128]{1,0:T(8,128)S(1)} %bitcast.18, s32[3,32,128]{2,1,0:T(8,128)S(1)} %get-tuple-element.14.ints_ref, ...), custom_call_target="tpu_custom_call" | custom-call | bytes 25165824 | tf_op jit(solution)/shard_map/add_inflow/pallas_call | solution.py:643
  (16 shorter events, 0.0 us)
Async XLA Ops:
  0.6 26.3 %copy-start = (s32[192,16]{0,1:T(8,128)S(1)}, s32[192,16]{0,1:T(8,128)}, u32[]{:S(2)}) copy-start(s32[192,16]{0,1:T(8,128)} %param.23) | copy-start | bytes 36868
  0.7 4.3 %copy-start.1 = (s32[1,1,16,256]{3,2,1,0:T(8,128)S(1)}, s32[1,1,16,256]{3,2,1,0:T(8,128)}, u32[]{:S(2)}) copy-start(s32[1,1,16,256]{3,2,1,0:T(8,128)} %cell_ref.1) | copy-start | bytes 49156
  0.7 4.3 %copy-start.2 = (s32[1,1,16,256]{3,2,1,0:T(8,128)S(1)}, s32[1,1,16,256]{3,2,1,0:T(8,128)}, u32[]{:S(2)}) copy-start(s32[1,1,16,256]{3,2,1,0:T(8,128)} %depth_ref.1) | copy-start | bytes 49156
  0.7 4.3 %copy-start.3 = (s32[1,1,16,256]{3,2,1,0:T(8,128)S(1)}, s32[1,1,16,256]{3,2,1,0:T(8,128)}, u32[]{:S(2)}) copy-start(s32[1,1,16,256]{3,2,1,0:T(8,128)} %seg_ref.1) | copy-start | bytes 49156
  0.7 4.3 %copy-start.4 = (f32[1,1,16,256]{3,2,1,0:T(8,128)S(1)}, f32[1,1,16,256]{3,2,1,0:T(8,128)}, u32[]{:S(2)}) copy-start(f32[1,1,16,256]{3,2,1,0:T(8,128)} %index_ref.1) | copy-start | bytes 49156
  0.7 4.3 %copy-start.5 = (s32[1,1,16]{2,1,0:T(1,128)S(1)}, s32[1,1,16]{2,1,0:T(1,128)}, u32[]{:S(2)}) copy-start(s32[1,1,16]{2,1,0:T(1,128)} %param.22) | copy-start | bytes 196
  4.2 47.4 %collective-permute-start = (f32[4,256,256]{2,1,0:T(8,128)}, f32[4,256,256]{2,1,0:T(8,128)S(1)}, u32[]{:S(2)}, u32[]{:S(2)}) collective-permute-start(f32[4,256,256]{2,1,0:T(8,128)} %get-tuple-element.16), channel_id=1, source_target_pairs={{0,1},{1,0},{2,3},{3,2},{4,5},{5,4},{6,7},{7,6},{8,9},{9,8},{10,11... | collective-permute-start | bytes 3145736 | tf_op jit(solution)/shard_map/ppermute | solution.py:708
  4.3 47.3 %collective-permute-start.1 = (f32[4,256,256]{2,1,0:T(8,128)S(1)}, f32[4,256,256]{2,1,0:T(8,128)S(1)}, u32[]{:S(2)}, u32[]{:S(2)}) collective-permute-start(f32[4,256,256]{2,1,0:T(8,128)S(1)} %get-tuple-element.17), channel_id=1, source_target_pairs={{1,2},{3,4},{5,6},{2,1},{4,3},{6,5},{9,10},{11,12},{13,14},{10,9},... | collective-permute-start | bytes 3145736 | tf_op jit(solution)/shard_map/ppermute | solution.py:712
  5.1 22.0 %copy-start.6 = (f32[192,16]{0,1:T(8,128)S(1)}, f32[192,16]{0,1:T(8,128)}, u32[]{:S(2)}) copy-start(f32[192,16]{0,1:T(8,128)} %param.25) | copy-start | bytes 36868
  5.1 22.0 %copy-start.7 = (f32[192,16]{0,1:T(8,128)S(1)}, f32[192,16]{0,1:T(8,128)}, u32[]{:S(2)}) copy-start(f32[192,16]{0,1:T(8,128)} %param.24) | copy-start | bytes 36868
  14.5 20.4 %all-to-all-start = ((f32[128,1,128]{2,1,0:T(1,128)}), f32[128,1,128]{2,1,0:T(1,128)S(1)}, u32[]{:S(2)}, u32[]{:S(2)}) async-start(f32[128,1,128]{2,1,0:T(1,128)} %bitcast.3), calls=%async_computation | async-start | bytes 131072 | tf_op jit(solution)/shard_map/all_to_all | solution.py:715
  35.9 35.5 %all-to-all-start.1 = ((f32[128,1,128]{2,1,0:T(1,128)}), f32[128,1,128]{2,1,0:T(1,128)S(1)}, u32[]{:S(2)}, u32[]{:S(2)}) async-start(f32[128,1,128]{2,1,0:T(1,128)} %bitcast.9), calls=%async_computation.1 | async-start | bytes 131072 | tf_op jit(solution)/shard_map/all_to_all | solution.py:715
  42.1 5.5 %collective-permute-start.2 = (f32[4,8,256]{2,1,0:T(8,128)S(1)}, f32[4,8,256]{2,1,0:T(8,128)S(1)}, u32[]{:S(2)}, u32[]{:S(2)}) collective-permute-start(f32[4,8,256]{2,1,0:T(8,128)S(1)} %get-tuple-element.18), channel_id=1, source_target_pairs={{0,8},{8,0},{16,24},{24,16},{32,40},{40,32},{48,56},{56,48},{64,72... | collective-permute-start | bytes 98312 | tf_op jit(solution)/shard_map/ppermute | solution.py:708
  43.7 7.9 %collective-permute-start.3 = (f32[4,8,256]{2,1,0:T(8,128)S(1)}, f32[4,8,256]{2,1,0:T(8,128)S(1)}, u32[]{:S(2)}, u32[]{:S(2)}) collective-permute-start(f32[4,8,256]{2,1,0:T(8,128)S(1)} %get-tuple-element.19), channel_id=1, source_target_pairs={{8,16},{24,32},{40,48},{56,64},{72,80},{88,96},{104,112},{16,8},{3... | collective-permute-start | bytes 98312 | tf_op jit(solution)/shard_map/ppermute | solution.py:712
where the time goes:
time: 82.3 us; the launch traced here: 82.1 us
  Pallas kernels  44.3 us (54%)
  starting transfers between devices  24.9 us (30%)
  waiting for transfers between devices  11.7 us (14%)
    pallas_call x2, Pallas kernels, cell_flows(): pl.pallas_call(functools.partial(flow_kernel, z0, nz), grid=(nz,), in_spe...  19.9 us
    all_to_all x2, starting transfers between devices, exchange(): lax.all_to_all(values, ('areal', 'layer'), split_axis=0, concat_axis=0, t...  18.6 us
    pallas_call x1, Pallas kernels, add_inflow(): pl.pallas_call(inflow_kernel, grid_spec=pltpu.PrefetchScalarGridSpec(num_...  10.6 us
    pallas_call x1, Pallas kernels, gather_sums(): pl.pallas_call(gather_kernel, in_specs=[pl.BlockSpec(memory_space=pltpu.S...  9.41 us
    all_to_all x2, waiting for transfers between devices, exchange(): lax.all_to_all(values, ('areal', 'layer'), split_axis=0, concat_axis=0, t...  7.77 us
    ppermute x2, starting transfers between devices, odd_swap(): return lax.ppermute(values, axis, pairs + [(j, i) for i, j in pairs])  4.69 us
    ppermute x2, waiting for transfers between devices, odd_swap(): return lax.ppermute(values, axis, pairs + [(j, i) for i, j in pairs])  3.92 us
    pallas_call x1, Pallas kernels, pack_halos(): pl.pallas_call(pack_kernel, in_specs=[pl.BlockSpec(memory_space=pltpu.SME...  3.43 us
  transfers between devices with their start and end apart: 6, of which 2 were waited for; matrix products, arithmetic and copies ran while one was open for 0% of the time, Pallas kernels for 37%

commit v1 on v0

--- a/solution.py
+++ b/solution.py
@@ -1,5 +1,3 @@
-import functools
-
 import jax
 import jax.numpy as jnp
 from jax import lax
@@ -23,7 +21,6 @@
 GROUP = WELLS_DEV // N_LAYER
 HALF = 32
 UNROLL = 4
-VMEM_KERNEL = 26 << 20
 
 MU_WATER = 0.5
 MU_OIL = 2.0
@@ -49,6 +46,10 @@
     return pltpu.with_memory_space_constraint(value, pltpu.HBM)
 
 
+def in_vmem(value):
+    return pltpu.with_memory_space_constraint(value, pltpu.VMEM)
+
+
 def iota(shape, dim):
     return lax.broadcasted_iota(I32, shape, dim)
 
@@ -58,31 +59,10 @@
 
 
 def gather_kernel(
-    blocks_s, p_hbm, sat_hbm, cell_ref, depth_ref, seg_ref, index_ref,
-    sums_ref, rows_ref, ints_ref, floats_ref, p_rows, sat_rows, m_rows, p_groups, m_groups, rows_s, sem, sems
+    blocks_s, p_ref, sat_ref, cell_ref, depth_ref, seg_ref, index_ref,
+    sums_ref, rows_ref, ints_ref, floats_ref, p_rows, m_rows, p_groups, m_groups, rows_s, sem
 ):
     to_smem = pltpu.make_async_copy(rows_ref, rows_s, sem)
-    copies = []
-    for z in range(CZ):
-        for half in range(2):
-            cols = pl.ds(half * LANES, LANES)
-            at = pl.ds(half * ROWS + z * CX, CX)
-            copies.append(
-                [
-                    pltpu.make_async_copy(
-                        sat_hbm.at[0, z, :, cols], sat_rows.at[0, at, :], sems.at[z, half, 0]
-                    ),
-                    pltpu.make_async_copy(
-                        sat_hbm.at[1, z, :, cols], sat_rows.at[1, at, :], sems.at[z, half, 1]
-                    ),
-                    pltpu.make_async_copy(
-                        p_hbm.at[z, :, cols], p_rows.at[at, :], sems.at[z, half, 2]
-                    ),
-                ]
-            )
-            for copy in copies[-1]:
-                copy.start()
-
     for half in range(2):
         cols = slice(half * LANES, (half + 1) * LANES)
         here = slice(half * OWNERS, (half + 1) * OWNERS)
@@ -101,19 +81,21 @@
         floats_ref[0, here, :] = index_ref[0, 0, :, cols]
     to_smem.start()
 
-    for z in range(CZ):
+    def dense(i, carry):
+        z = lax.div(i, CX // 32)
+        row = pl.multiple_of((i - z * (CX // 32)) * 32, 32)
+        here = pl.ds(row, 32)
+        press = p_ref[z, here, :]
+        lam = mobilities(sat_ref[0, z, here, :], sat_ref[1, z, here, :])
+        total = lam[0] + lam[1] + lam[2]
         for half in range(2):
-            for copy in copies[2 * z + half]:
-                copy.wait()
-
-            def dense(i, carry):
-                at = pl.ds(pl.multiple_of(half * ROWS + z * CX + 64 * i, 64), 64)
-                lam = mobilities(sat_rows[0, at, :], sat_rows[1, at, :])
-                m_rows[at, :] = lam[0] + lam[1] + lam[2]
-                return carry
-
-            lax.fori_loop(0, CX // 64, dense, 0)
-
+            at = pl.ds(pl.multiple_of(half * ROWS + 32 * i, 32), 32)
+            cols = slice(half * LANES, (half + 1) * LANES)
+            p_rows[at, :] = press[:, cols]
+            m_rows[at, :] = total[:, cols]
+        return carry
+
+    lax.fori_loop(0, CZ * CX // 32, dense, 0)
     to_smem.wait()
     sub = iota((8, LANES), 0)
     lane = iota((8, LANES), 1)
@@ -187,11 +169,10 @@
 
 
 def gather_sums(blocks, pressure, saturations, cell, depth, seg, index):
-    hbm = pl.BlockSpec(memory_space=pl.ANY)
     vmem = pl.BlockSpec(memory_space=pltpu.VMEM)
     return pl.pallas_call(
         gather_kernel,
-        in_specs=[pl.BlockSpec(memory_space=pltpu.SMEM), hbm, hbm] + [vmem] * 4,
+        in_specs=[pl.BlockSpec(memory_space=pltpu.SMEM)] + [vmem] * 6,
         out_specs=[vmem] * 4,
         out_shape=[
             jax.ShapeDtypeStruct((DEVICES, LANES), F32),
@@ -201,18 +182,16 @@
         ],
         scratch_shapes=[
             pltpu.VMEM((2 * ROWS, LANES), F32),
-            pltpu.VMEM((2, 2 * ROWS, LANES), F32),
             pltpu.VMEM((2 * ROWS, LANES), F32),
             pltpu.VMEM((2 * OWNERS, LANES, LANES), F32),
             pltpu.VMEM((2 * OWNERS, LANES, LANES), F32),
             pltpu.SMEM((2 * OWNERS, LANES), I32),
             pltpu.SemaphoreType.DMA(()),
-            pltpu.SemaphoreType.DMA((CZ, 2, 3)),
         ],
-        compiler_params=pltpu.CompilerParams(vmem_limit_bytes=VMEM_KERNEL),
+        compiler_params=pltpu.CompilerParams(vmem_limit_bytes=10 << 20),
         cost_estimate=pl.CostEstimate(flops=0, bytes_accessed=24 << 20, transcendentals=0),
         name="gather_sums",
-    )(blocks, in_hbm(pressure), in_hbm(saturations), cell, depth, seg, index)
+    )(blocks, in_vmem(pressure), in_vmem(saturations), cell, depth, seg, index)
 
 
 def pack_kernel(
@@ -258,8 +237,8 @@
         in_specs=[pl.BlockSpec(memory_space=pltpu.SMEM)] + [hbm] * 3,
         out_specs=[vmem] * 4,
         out_shape=[
-            jax.ShapeDtypeStruct((4, CX, CY), F32),
-            jax.ShapeDtypeStruct((4, CX, CY), F32),
+            pltpu.VMEM((4, CX, CY), F32),
+            pltpu.VMEM((4, CX, CY), F32),
             jax.ShapeDtypeStruct((4, CZ, CY), F32),
             jax.ShapeDtypeStruct((4, CZ, CY), F32),
         ],
@@ -267,7 +246,7 @@
             pltpu.VMEM((2, 4, CZ, 8, CY), F32),
             pltpu.SemaphoreType.DMA((4, 4)),
         ],
-        compiler_params=pltpu.CompilerParams(vmem_limit_bytes=VMEM_KERNEL),
+        compiler_params=pltpu.CompilerParams(vmem_limit_bytes=4 << 20),
         cost_estimate=pl.CostEstimate(flops=0, bytes_accessed=6 << 20, transcendentals=0),
         name="pack_halos",
     )(parity, in_hbm(pressure), in_hbm(saturations), in_hbm(permeability))
@@ -351,17 +330,13 @@
 
 
 def flow_kernel(
-    z0, nz, parity_s, p_hbm, sat_hbm, k_hbm, plane_even_ref, plane_odd_ref, row_even_ref, row_odd_ref,
+    parity_s, p_hbm, sat_hbm, k_hbm, plane_even_ref, plane_odd_ref, row_even_ref, row_odd_ref,
     old_ref, pore_ref, out_ref,
     cells, lams, rolled, zflux, sems
 ):
-    step_at = pl.program_id(0)
-    layer = step_at + z0
-    now = lax.rem(step_at, 2)
+    layer = pl.program_id(0)
+    now = lax.rem(layer, 2)
     later = 1 - now
-    halo_below = z0 == 0
-    first_plane = z0 if halo_below else z0 - 1
-    last_plane = z0 + nz if halo_below else z0 + nz - 1
 
     def plane_copies(z):
         sources = (p_hbm.at[z], sat_hbm.at[0, z], sat_hbm.at[1, z], k_hbm.at[z])
@@ -393,12 +368,10 @@
             [cells[1, z, rows, :], cells[2, z, rows, :]],
         )
 
-    halo_from_even = parity_s[0] == (1 if halo_below else 0)
-
-    def halo_at(row, size):
+    def halo_at(from_even, row, size):
         rows = pl.ds(row, size)
         value = [
-            jnp.where(halo_from_even, plane_even_ref[f, rows, :], plane_odd_ref[f, rows, :])
+            jnp.where(from_even, plane_even_ref[f, rows, :], plane_odd_ref[f, rows, :])
             for f in range(4)
         ]
         return [value[0], value[3]], [value[1], value[2]]
@@ -409,19 +382,18 @@
             lams[now, a, rows, :] for a in range(3)
         ]
 
-    @pl.when(step_at == 0)
+    @pl.when(layer == 0)
     def _():
-        for z in range(first_plane, last_plane + 1):
+        for z in range(CZ):
             for copy in plane_copies(z):
                 copy.start()
-        for z in range(first_plane, z0 + 1):
-            for copy in plane_copies(z):
-                copy.wait()
+        for copy in plane_copies(0):
+            copy.wait()
 
         def first(i, carry):
             row = pl.multiple_of(STRIP * i, STRIP)
-            low, low_sat = halo_at(row, STRIP) if halo_below else cell_at(z0 - 1, row, STRIP)
-            high, high_sat = cell_at(z0, row, STRIP)
+            low, low_sat = halo_at(parity_s[0] == 1, row, STRIP)
+            high, high_sat = cell_at(0, row, STRIP)
             lam = doubled_mobilities(*high_sat)
             flux = vertical(low + list(doubled_mobilities(*low_sat)), high + list(lam))
             for a in range(3):
@@ -431,7 +403,6 @@
 
         lax.fori_loop(0, CX // STRIP, first, 0)
 
-    sub = iota((STRIP, CY), 0)
     top = iota((8, CY), 0) == 0
     last_lane = iota((STRIP, CY), 1) == CY - 1
 
@@ -443,7 +414,7 @@
         ]
         return [value[0], value[3]] + list(doubled_mobilities(value[1], value[2]))
 
-    east = side_row(parity_s[1] == 0)
+    east = [jnp.broadcast_to(v, (8, CY)) for v in side_row(parity_s[1] == 0)]
     flux = level(side_row(parity_s[1] == 1), [v[0:1] for v in here_at(0, 8)])
     down = tuple(jnp.broadcast_to(f, (8, CY)) for f in flux)
     for f, value in enumerate(here_at(0, STRIP)):
@@ -461,14 +432,11 @@
                 pl.multiple_of(jnp.minimum(row + STRIP, CX - STRIP), STRIP), STRIP
             )
             after_rolled = [pltpu.roll(v, CY - 1, 1) for v in after]
-            neighbour = [
-                jnp.where(
-                    sub == STRIP - 1,
-                    jnp.broadcast_to(jnp.where(final, e, n[0:1]), (STRIP, CY)),
-                    pltpu.roll(v, STRIP - 1, 0),
-                )
-                for v, n, e in zip(here, after, east)
-            ]
+            neighbour = []
+            for v, n, e in zip(here, after, east):
+                edge = jnp.where(final, e, n[0:8])
+                longer = jnp.concatenate([v, edge], axis=0)
+                neighbour.append(pltpu.roll(longer, STRIP + 7, 0)[0:STRIP])
             flux_x = level(here, neighbour)
             down_x = [pltpu.roll(f, 1, 0) for f in flux_x]
             heads = tuple(d[0:8] for d in down_x)
@@ -501,34 +469,30 @@
 
         lax.fori_loop(0, CX // STRIP, step, down)
 
-    inside = nz if halo_below else nz - 1
-
-    @pl.when(step_at < inside)
+    @pl.when(layer < CZ - 1)
     def _():
         for copy in plane_copies(layer + 1):
             copy.wait()
         sweep(lambda row, size: cell_at(layer + 1, row, size))
 
-    if not halo_below:
-
-        @pl.when(step_at == inside)
-        def _():
-            sweep(halo_at)
-
-
-def cell_flows(z0, nz, parity, pressure, saturations, permeability, planes, sides, old, pore):
+    @pl.when(layer == CZ - 1)
+    def _():
+        sweep(lambda row, size: halo_at(parity_s[0] == 0, row, size))
+
+
+def cell_flows(parity, pressure, saturations, permeability, planes, sides, old, pore):
     hbm = pl.BlockSpec(memory_space=pl.ANY)
     vmem = pl.BlockSpec(memory_space=pltpu.VMEM)
     return pl.pallas_call(
-        functools.partial(flow_kernel, z0, nz),
-        grid=(nz,),
+        flow_kernel,
+        grid=(CZ,),
         in_specs=[pl.BlockSpec(memory_space=pltpu.SMEM), hbm, hbm, hbm, vmem, vmem, vmem, vmem]
         + [
-            pl.BlockSpec((2, 1, CX, CY), lambda z: (0, z + z0, 0, 0)),
-            pl.BlockSpec((1, CX, CY), lambda z: (z + z0, 0, 0)),
+            pl.BlockSpec((2, 1, CX, CY), lambda z: (0, z, 0, 0)),
+            pl.BlockSpec((1, CX, CY), lambda z: (z, 0, 0)),
         ],
         out_specs=pl.BlockSpec((3, 1, CX, CY), lambda z: (0, z, 0, 0)),
-        out_shape=pltpu.HBM((3, nz, CX, CY), F32),
+        out_shape=pltpu.HBM((3, CZ, CX, CY), F32),
         scratch_shapes=[
             pltpu.VMEM((4, CZ, CX, CY), F32),
             pltpu.VMEM((2, 3, CX, CY), F32),
@@ -536,22 +500,23 @@
             pltpu.VMEM((3, CX, CY), F32),
             pltpu.SemaphoreType.DMA((CZ, 4)),
         ],
-        compiler_params=pltpu.CompilerParams(vmem_limit_bytes=VMEM_KERNEL),
+        compiler_params=pltpu.CompilerParams(vmem_limit_bytes=16 << 20),
         cost_estimate=pl.CostEstimate(flops=0, bytes_accessed=20 << 20, transcendentals=0),
+        name="cell_flows",
     )(
         parity, in_hbm(pressure), in_hbm(saturations), in_hbm(permeability), *planes, *sides, in_hbm(old), in_hbm(pore)
     )
 
 
 def inflow_kernel(
-    rows_s, blocks_s, areal_s, pw_ref, ints_ref, floats_ref, low_hbm, high_hbm, sat_hbm,
+    rows_s, blocks_s, areal_s, pw_ref, ints_ref, floats_ref, flow_hbm, sat_hbm,
     out_ref, slab_ref, rate, flows, sats, sems, *sums
 ):
     layer = pl.program_id(0)
 
-    def layer_copies(source, at, z):
+    def layer_copies(z):
         return [
-            pltpu.make_async_copy(source.at[a, at], flows.at[a, z], sems.at[z, a]) for a in range(3)
+            pltpu.make_async_copy(flow_hbm.at[a, z], flows.at[a, z], sems.at[z, a]) for a in range(3)
         ] + [
             pltpu.make_async_copy(sat_hbm.at[a, z], sats.at[a, z], sems.at[z, 3 + a]) for a in range(2)
         ]
@@ -559,8 +524,7 @@
     @pl.when(layer == 0)
     def _():
         for z in range(CZ):
-            source = low_hbm if z < CZ // 2 else high_hbm
-            for copy in layer_copies(source, z % (CZ // 2), z):
+            for copy in layer_copies(z):
                 copy.start()
         zero = jnp.zeros((64, LANES), F32)
 
@@ -619,7 +583,7 @@
 
         lax.fori_loop(0, OWNERS, owner_step, 0)
 
-    for copy in layer_copies(low_hbm, 0, layer):
+    for copy in layer_copies(layer):
         copy.wait()
 
     def combine(i, carry):
@@ -637,7 +601,7 @@
     lax.fori_loop(0, CX // 32, combine, 0)
 
 
-def add_inflow(rows, blocks, areal, pw, ints, floats, low, high, saturations):
+def add_inflow(rows, blocks, areal, pw, ints, floats, flow, saturations):
     hbm = pl.BlockSpec(memory_space=pl.ANY)
     flow_spec = pl.BlockSpec((3, 1, CX, CY), lambda z, *_: (0, z, 0, 0))
     return pl.pallas_call(
@@ -649,7 +613,6 @@
                 pl.BlockSpec((DEVICES, LANES), lambda z, *_: (0, 0)),
                 pl.BlockSpec((3, 2 * OWNERS, LANES), lambda z, *_: (0, 0, 0)),
                 pl.BlockSpec((2, 2 * OWNERS, LANES), lambda z, *_: (0, 0, 0)),
-                hbm,
                 hbm,
                 hbm,
             ],
@@ -666,10 +629,10 @@
             jax.ShapeDtypeStruct((3, CZ, CX, CY), F32),
             jax.ShapeDtypeStruct((SEG_SLAB, WELLS_DEV), F32),
         ],
-        compiler_params=pltpu.CompilerParams(vmem_limit_bytes=VMEM_KERNEL),
+        compiler_params=pltpu.CompilerParams(vmem_limit_bytes=24 << 20),
         cost_estimate=pl.CostEstimate(flops=0, bytes_accessed=24 << 20, transcendentals=0),
         name="add_inflow",
-    )(rows, blocks, areal, pw, ints, floats, in_hbm(low), in_hbm(high), in_hbm(saturations))
+    )(rows, blocks, areal, pw, ints, floats, in_hbm(flow), in_hbm(saturations))
 
 
 def on_device(
@@ -692,18 +655,12 @@
     layer = lax.axis_index("layer").astype(I32)
     areal = lax.axis_index("areal").astype(I32).reshape(1)
     blocks = perf_blocks[0, 0]
-    depth = CZ // 2
     parity = jnp.concatenate([layer.reshape(1), areal]) & 1
 
     def own_wells(values):
         part = lax.dynamic_slice_in_dim(values, layer * GROUP, GROUP, axis=0)
         return jnp.pad(part.T, ((0, 0), (0, LANES - GROUP)))
 
-    def flows(z0):
-        return cell_flows(
-            z0, depth, parity, pressure, saturations, permeability, planes, sides, old_saturations, pore_volume
-        )
-
     def even_swap(values, axis, count):
         return lax.ppermute(values, axis, [(i, i ^ 1) for i in range(count)])
 
@@ -715,21 +672,24 @@
         return lax.all_to_all(values, ("areal", "layer"), split_axis=0, concat_axis=0, tiled=True)
 
     packed = pack_halos(parity, pressure, saturations, permeability)
+    sums, rows, ints, floats = gather_sums(
+        blocks, pressure, saturations, perf_cell, perf_layer, perf_seg, perf_index
+    )
+    received = exchange(sums)
     plane_even = even_swap(packed[0], "layer", n_layer)
     plane_odd = odd_swap(packed[1], "layer", n_layer)
     row_even = even_swap(packed[2], "areal", n_areal)
     row_odd = odd_swap(packed[3], "areal", n_areal)
     planes, sides = (plane_even, plane_odd), (row_even, row_odd)
-    sums, rows, ints, floats = gather_sums(
-        blocks, pressure, saturations, perf_cell, perf_layer, perf_seg, perf_index
-    )
-    received = exchange(sums)
-    low = flows(0)
     systems = [own_wells(v) for v in (seg_parent, seg_cond, seg_target)]
     solved = solve_wells(received, *systems)
     pw = exchange(solved)
-    high = flows(depth)
-    residual, slab = add_inflow(rows, blocks, areal, pw, ints, floats, low, high, saturations)
+    flow = cell_flows(
+        parity, pressure, saturations, permeability, planes, sides, old_saturations, pore_volume
+    )
+    residual, slab = add_inflow(
+        rows, blocks, areal, pw, ints, floats, flow, saturations
+    )
     return residual, slab.T
 
 

time: 82.3 us -> 77.2 us (0.938)
  Pallas kernels: 44.3 us -> 39.1 us
    pallas_call x2 -> x1, Pallas kernels: 19.9 us -> 15.9 us  [cell_flows(): pl.pallas_call(flow_kernel, grid=(CZ,), in_specs=[pl.BlockSpec(memory_spa...]
    pallas_call x1, Pallas kernels: 9.41 us -> 7.53 us  [gather_sums(): pl.pallas_call(gather_kernel, in_specs=[pl.BlockSpec(memory_space=pltpu.S...]
    ppermute x2, starting transfers between devices: 4.69 us -> 5.62 us  [odd_swap(): return lax.ppermute(values, axis, pairs + [(j, i) for i, j in pairs])]
    all_to_all x2, starting transfers between devices: 18.6 us -> 17.7 us  [exchange(): lax.all_to_all(values, ('areal', 'layer'), split_axis=0, concat_axis=0, t...]
  transfers between devices with their start and end apart: 6 -> 6, of which waited for: 2 -> 2; matrix products, arithmetic and copies ran while one was open for 0% -> 0% of each run, Pallas kernels for 37% -> 32%
where the time goes in v1:
time: 77.2 us; the launch traced here: 76.8 us
  Pallas kernels  39.1 us (51%)
  starting transfers between devices  24.9 us (32%)
  waiting for transfers between devices  11.7 us (15%)
  between operations  0.8 us (1%)
    all_to_all x2, starting transfers between devices, exchange(): lax.all_to_all(values, ('areal', 'layer'), split_axis=0, concat_axis=0, t...  17.7 us
    pallas_call x1, Pallas kernels, cell_flows(): pl.pallas_call(flow_kernel, grid=(CZ,), in_specs=[pl.BlockSpec(memory_spa...  15.9 us
    pallas_call x1, Pallas kernels, add_inflow(): pl.pallas_call(inflow_kernel, grid_spec=pltpu.PrefetchScalarGridSpec(num_...  10.6 us
    all_to_all x2, waiting for transfers between devices, exchange(): lax.all_to_all(values, ('areal', 'layer'), split_axis=0, concat_axis=0, t...  7.77 us
    pallas_call x1, Pallas kernels, gather_sums(): pl.pallas_call(gather_kernel, in_specs=[pl.BlockSpec(memory_space=pltpu.S...  7.53 us
    ppermute x2, starting transfers between devices, odd_swap(): return lax.ppermute(values, axis, pairs + [(j, i) for i, j in pairs])  5.62 us
    pallas_call x1, Pallas kernels, pack_halos(): pl.pallas_call(pack_kernel, in_specs=[pl.BlockSpec(memory_space=pltpu.SME...  4.06 us
    ppermute x2, waiting for transfers between devices, odd_swap(): return lax.ppermute(values, axis, pairs + [(j, i) for i, j in pairs])  3.92 us
  transfers between devices with their start and end apart: 6, of which 2 were waited for; matrix products, arithmetic and copies ran while one was open for 0% of the time, Pallas kernels for 32%

profile of v1, /device:TPU:4, one launch (start us, length us, event | category | flops | bytes accessed | tf_op | source)
XLA Modules:
  0.0 76.8 jit_solution(2184397860962530122)
XLA Ops:
  0.6 0.0 copy-start
  0.6 0.1 add_and_fusion.parity_s
  0.7 0.0 copy-start.5
  0.7 0.0 copy-start.6
  0.8 0.0 copy-start.7
  0.8 4.1 %pack_halos.1 = (f32[4,256,256]{2,1,0:T(8,128)}, f32[4,256,256]{2,1,0:T(8,128)}, f32[4,8,256]{2,1,0:T(8,128)S(1)}, f32[4,8,256]{2,1,0:T(8,128)S(1)}) custom-call(s32[2]{0:T(128)S(1)} %add_and_fusion.parity_s, f32[8,256,256]{2,1,0:T(8,128)} %p_hbm.3, f32[2,8,256,256]{3,2,1,0:T(8,128)} %sat_hbm.5, f32[8,256,256]{2,1,0:T(8,128)} %k_hbm.3), custom_call_target="tpu_custom_call" | custom-call | bytes 6291456 | tf_op jit(solution)/shard_map/pack_halos/pallas_call | solution.py:235
  4.8 0.0 copy-start.8
  4.8 0.0 copy-start.9
  4.9 0.1 collective-permute-start
  5.0 1.6 %collective-permute-start.1 = (f32[4,256,256]{2,1,0:T(8,128)}, f32[4,256,256]{2,1,0:T(8,128)}, u32[]{:S(2)}, u32[]{:S(2)}) collective-permute-start(f32[4,256,256]{2,1,0:T(8,128)} %get-tuple-element.17), channel_id=1, source_target_pairs={{1,2},{3,4},{5,6},{2,1},{4,3},{6,5},{9,10},{11,12},{13,14},{10,9},... | collective-permute-start | bytes 3145736 | tf_op jit(solution)/shard_map/ppermute | solution.py:669
  6.6 7.5 %gather_sums.1 = (f32[128,128]{1,0:T(8,128)}, s32[32,128]{1,0:T(8,128)S(1)}, s32[3,32,128]{2,1,0:T(8,128)S(1)}, f32[2,32,128]{2,1,0:T(8,128)S(1)}) custom-call(s32[16]{0:T(128)S(1)} %bitcast.20, f32[8,256,256]{2,1,0:T(8,128)S(1)} %copy-done.2, f32[2,8,256,256]{3,2,1,0:T(8,128)S(1)} %copy-done.1, s32[1,1,16,256]{3,2,1,0:T(8,128)S(1)} %copy-done.3, ...), custom_call_target="tpu_custom_call" | custom-call | bytes 25165824 | tf_op jit(solution)/shard_map/gather_sums/pallas_call | solution.py:173
  14.2 11.5 %all-to-all-start = ((f32[128,1,128]{2,1,0:T(1,128)}), f32[128,1,128]{2,1,0:T(1,128)S(1)}, u32[]{:S(2)}, u32[]{:S(2)}) async-start(f32[128,1,128]{2,1,0:T(1,128)} %bitcast.3), calls=%async_computation | async-start | bytes 131072 | tf_op jit(solution)/shard_map/all_to_all | solution.py:672
  25.7 0.1 dynamic-slice_bitcast_fusion.2
  25.8 0.1 dynamic-slice_bitcast_fusion
  25.9 7.8 %all-to-all-done = f32[128,1,128]{2,1,0:T(1,128)S(1)} async-done(((f32[128,1,128]{2,1,0:T(1,128)}), f32[128,1,128]{2,1,0:T(1,128)S(1)}, u32[]{:S(2)}, u32[]{:S(2)}) %all-to-all-start) | async-done | bytes 65568 | tf_op jit(solution)/shard_map/all_to_all | solution.py:672
  33.7 1.0 %solve_wells.1 = f32[128,128]{1,0:T(8,128)} custom-call(f32[128,128]{1,0:T(8,128)S(1)} %bitcast.19, s32[16,128]{1,0:T(8,128)S(1)} %pad.11.parent_ref, f32[16,128]{1,0:T(8,128)S(1)} %pad.12.cond_ref, f32[16,128]{1,0:T(8,128)S(1)} %pad.13.target_ref), custom_call_target="tpu_custom_call" | custom-call | bytes 1048576 | tf_op jit(solution)/shard_map/solve_wells/pallas_call | solution.py:297
  34.7 6.2 %all-to-all-start.1 = ((f32[128,1,128]{2,1,0:T(1,128)}), f32[128,1,128]{2,1,0:T(1,128)S(1)}, u32[]{:S(2)}, u32[]{:S(2)}) async-start(f32[128,1,128]{2,1,0:T(1,128)} %bitcast.9), calls=%async_computation.1 | async-start | bytes 131072 | tf_op jit(solution)/shard_map/all_to_all | solution.py:672
  40.9 1.5 %collective-permute-start.2 = (f32[4,8,256]{2,1,0:T(8,128)S(1)}, f32[4,8,256]{2,1,0:T(8,128)S(1)}, u32[]{:S(2)}, u32[]{:S(2)}) collective-permute-start(f32[4,8,256]{2,1,0:T(8,128)S(1)} %get-tuple-element.18), channel_id=1, source_target_pairs={{0,8},{8,0},{16,24},{24,16},{32,40},{40,32},{48,56},{56,48},{64,72... | collective-permute-start | bytes 98312 | tf_op jit(solution)/shard_map/ppermute | solution.py:665
  42.4 4.0 %collective-permute-start.3 = (f32[4,8,256]{2,1,0:T(8,128)S(1)}, f32[4,8,256]{2,1,0:T(8,128)S(1)}, u32[]{:S(2)}, u32[]{:S(2)}) collective-permute-start(f32[4,8,256]{2,1,0:T(8,128)S(1)} %get-tuple-element.19), channel_id=1, source_target_pairs={{8,16},{24,32},{40,48},{56,64},{72,80},{88,96},{104,112},{16,8},{3... | collective-permute-start | bytes 98312 | tf_op jit(solution)/shard_map/ppermute | solution.py:669
  46.4 0.0 collective-permute-done.2.row_even_ref
  46.4 3.9 %collective-permute-done.3.row_odd_ref = f32[4,8,256]{2,1,0:T(8,128)S(1)} collective-permute-done((f32[4,8,256]{2,1,0:T(8,128)S(1)}, f32[4,8,256]{2,1,0:T(8,128)S(1)}, u32[]{:S(2)}, u32[]{:S(2)}) %collective-permute-start.3) | collective-permute-done | bytes 32800 | tf_op jit(solution)/shard_map/ppermute | solution.py:669
  50.4 15.9 %cell_flows.1.flow_hbm = f32[3,8,256,256]{3,2,1,0:T(8,128)} custom-call(s32[2]{0:T(128)S(1)} %add_and_fusion.parity_s, f32[8,256,256]{2,1,0:T(8,128)} %p_hbm.3, f32[2,8,256,256]{3,2,1,0:T(8,128)} %sat_hbm.5, f32[8,256,256]{2,1,0:T(8,128)} %k_hbm.3, f32[4,256,256]{2,1,0:T(8,128)S(1)} %collective-permute-done.plane_even_ref, ...), custom_call_target="tpu_custom_call" | custom-call | bytes 20971520 | tf_op jit(solution)/shard_map/cell_flows/pallas_call | solution.py:486
  66.2 0.0 all-to-all-done.1
  66.2 10.6 %add_inflow.1 = (f32[3,8,256,256]{3,2,1,0:T(8,128)}, f32[2,192]{1,0:T(2,128)}) custom-call(s32[32,128]{1,0:T(8,128)S(1)} %get-tuple-element.12.rows_s, s32[16]{0:T(128)S(1)} %bitcast.21, s32[1]{0:T(128)} %bitcast.1.areal_s, f32[128,128]{1,0:T(8,128)S(1)} %bitcast.18, s32[3,32,128]{2,1,0:T(8,128)S(1)} %get-tuple-element.14.ints_ref, ...), custom_call_target="tpu_custom_call" | custom-call | bytes 25165824 | tf_op jit(solution)/shard_map/add_inflow/pallas_call | solution.py:607
  (19 shorter events, 0.0 us)
Async XLA Ops:
  0.6 25.1 %copy-start = (s32[192,16]{0,1:T(8,128)S(1)}, s32[192,16]{0,1:T(8,128)}, u32[]{:S(2)}) copy-start(s32[192,16]{0,1:T(8,128)} %param.23) | copy-start | bytes 36868
  0.7 5.9 %copy-start.1 = (f32[2,8,256,256]{3,2,1,0:T(8,128)S(1)}, f32[2,8,256,256]{3,2,1,0:T(8,128)}, u32[]{:S(2)}) copy-start(f32[2,8,256,256]{3,2,1,0:T(8,128)} %sat_hbm.5) | copy-start | bytes 12582916
  0.7 5.9 %copy-start.2 = (f32[8,256,256]{2,1,0:T(8,128)S(1)}, f32[8,256,256]{2,1,0:T(8,128)}, u32[]{:S(2)}) copy-start(f32[8,256,256]{2,1,0:T(8,128)} %p_hbm.3) | copy-start | bytes 6291460
  0.7 5.9 %copy-start.3 = (s32[1,1,16,256]{3,2,1,0:T(8,128)S(1)}, s32[1,1,16,256]{3,2,1,0:T(8,128)}, u32[]{:S(2)}) copy-start(s32[1,1,16,256]{3,2,1,0:T(8,128)} %cell_ref.1) | copy-start | bytes 49156
  0.7 5.9 %copy-start.4 = (s32[1,1,16,256]{3,2,1,0:T(8,128)S(1)}, s32[1,1,16,256]{3,2,1,0:T(8,128)}, u32[]{:S(2)}) copy-start(s32[1,1,16,256]{3,2,1,0:T(8,128)} %depth_ref.1) | copy-start | bytes 49156
  0.7 5.9 %copy-start.5 = (s32[1,1,16,256]{3,2,1,0:T(8,128)S(1)}, s32[1,1,16,256]{3,2,1,0:T(8,128)}, u32[]{:S(2)}) copy-start(s32[1,1,16,256]{3,2,1,0:T(8,128)} %seg_ref.1) | copy-start | bytes 49156
  0.7 5.9 %copy-start.6 = (f32[1,1,16,256]{3,2,1,0:T(8,128)S(1)}, f32[1,1,16,256]{3,2,1,0:T(8,128)}, u32[]{:S(2)}) copy-start(f32[1,1,16,256]{3,2,1,0:T(8,128)} %index_ref.1) | copy-start | bytes 49156
  0.8 5.9 %copy-start.7 = (s32[1,1,16]{2,1,0:T(1,128)S(1)}, s32[1,1,16]{2,1,0:T(1,128)}, u32[]{:S(2)}) copy-start(s32[1,1,16]{2,1,0:T(1,128)} %param.22) | copy-start | bytes 196
  4.8 21.0 %copy-start.8 = (f32[192,16]{0,1:T(8,128)S(1)}, f32[192,16]{0,1:T(8,128)}, u32[]{:S(2)}) copy-start(f32[192,16]{0,1:T(8,128)} %param.25) | copy-start | bytes 36868
  4.8 21.0 %copy-start.9 = (f32[192,16]{0,1:T(8,128)S(1)}, f32[192,16]{0,1:T(8,128)}, u32[]{:S(2)}) copy-start(f32[192,16]{0,1:T(8,128)} %param.24) | copy-start | bytes 36868
  4.9 45.5 %collective-permute-start = (f32[4,256,256]{2,1,0:T(8,128)}, f32[4,256,256]{2,1,0:T(8,128)S(1)}, u32[]{:S(2)}, u32[]{:S(2)}) collective-permute-start(f32[4,256,256]{2,1,0:T(8,128)} %get-tuple-element.16), channel_id=1, source_target_pairs={{0,1},{1,0},{2,3},{3,2},{4,5},{5,4},{6,7},{7,6},{8,9},{9,8},{10,11... | collective-permute-start | bytes 3145736 | tf_op jit(solution)/shard_map/ppermute | solution.py:665
  5.0 45.4 %collective-permute-start.1 = (f32[4,256,256]{2,1,0:T(8,128)}, f32[4,256,256]{2,1,0:T(8,128)}, u32[]{:S(2)}, u32[]{:S(2)}) collective-permute-start(f32[4,256,256]{2,1,0:T(8,128)} %get-tuple-element.17), channel_id=1, source_target_pairs={{1,2},{3,4},{5,6},{2,1},{4,3},{6,5},{9,10},{11,12},{13,14},{10,9},... | collective-permute-start | bytes 3145736 | tf_op jit(solution)/shard_map/ppermute | solution.py:669
  14.2 19.5 %all-to-all-start = ((f32[128,1,128]{2,1,0:T(1,128)}), f32[128,1,128]{2,1,0:T(1,128)S(1)}, u32[]{:S(2)}, u32[]{:S(2)}) async-start(f32[128,1,128]{2,1,0:T(1,128)} %bitcast.3), calls=%async_computation | async-start | bytes 131072 | tf_op jit(solution)/shard_map/all_to_all | solution.py:672
  34.7 31.5 %all-to-all-start.1 = ((f32[128,1,128]{2,1,0:T(1,128)}), f32[128,1,128]{2,1,0:T(1,128)S(1)}, u32[]{:S(2)}, u32[]{:S(2)}) async-start(f32[128,1,128]{2,1,0:T(1,128)} %bitcast.9), calls=%async_computation.1 | async-start | bytes 131072 | tf_op jit(solution)/shard_map/all_to_all | solution.py:672
  40.9 5.5 %collective-permute-start.2 = (f32[4,8,256]{2,1,0:T(8,128)S(1)}, f32[4,8,256]{2,1,0:T(8,128)S(1)}, u32[]{:S(2)}, u32[]{:S(2)}) collective-permute-start(f32[4,8,256]{2,1,0:T(8,128)S(1)} %get-tuple-element.18), channel_id=1, source_target_pairs={{0,8},{8,0},{16,24},{24,16},{32,40},{40,32},{48,56},{56,48},{64,72... | collective-permute-start | bytes 98312 | tf_op jit(solution)/shard_map/ppermute | solution.py:665
  42.4 7.9 %collective-permute-start.3 = (f32[4,8,256]{2,1,0:T(8,128)S(1)}, f32[4,8,256]{2,1,0:T(8,128)S(1)}, u32[]{:S(2)}, u32[]{:S(2)}) collective-permute-start(f32[4,8,256]{2,1,0:T(8,128)S(1)} %get-tuple-element.19), channel_id=1, source_target_pairs={{8,16},{24,32},{40,48},{56,64},{72,80},{88,96},{104,112},{16,8},{3... | collective-permute-start | bytes 98312 | tf_op jit(solution)/shard_map/ppermute | solution.py:669

commit v2 on v1

--- a/solution.py
+++ b/solution.py
@@ -15,6 +15,7 @@
 SEG = 16
 SEG_SLAB = 2
 OWNERS = 16
+SLOTS = 256
 ACCS = 4
 N_LAYER = 8
 DEVICES = OWNERS * N_LAYER
@@ -46,10 +47,6 @@
     return pltpu.with_memory_space_constraint(value, pltpu.HBM)
 
 
-def in_vmem(value):
-    return pltpu.with_memory_space_constraint(value, pltpu.VMEM)
-
-
 def iota(shape, dim):
     return lax.broadcasted_iota(I32, shape, dim)
 
@@ -59,43 +56,86 @@
 
 
 def gather_kernel(
-    blocks_s, p_ref, sat_ref, cell_ref, depth_ref, seg_ref, index_ref,
-    sums_ref, rows_ref, ints_ref, floats_ref, p_rows, m_rows, p_groups, m_groups, rows_s, sem
+    blocks_s, parity_s, p_hbm, sat_hbm, k_hbm, cell_hbm, depth_hbm, seg_hbm, index_hbm,
+    sums_ref, rows_ref, ints_ref, floats_ref, plane_even_hbm, plane_odd_hbm, row_even_ref, row_odd_ref,
+    p_cells, sat_cells, p_rows, m_rows, p_groups, m_groups, rows_s, edges, planes, slots, index_slots,
+    sem, sems, edge_sems, plane_sems, slot_sems
 ):
     to_smem = pltpu.make_async_copy(rows_ref, rows_s, sem)
+    slots_in = [
+        pltpu.make_async_copy(source.at[0, 0], slots.at[f], slot_sems.at[f])
+        for f, source in enumerate((cell_hbm, depth_hbm, seg_hbm))
+    ] + [pltpu.make_async_copy(index_hbm.at[0, 0], index_slots, slot_sems.at[3])]
+    for copy in slots_in:
+        copy.start()
+    copies = []
+    for z in range(CZ):
+        copies.append(
+            [
+                pltpu.make_async_copy(p_hbm.at[z], p_cells.at[z], sems.at[z, 0]),
+                pltpu.make_async_copy(sat_hbm.at[0, z], sat_cells.at[0, z], sems.at[z, 1]),
+                pltpu.make_async_copy(sat_hbm.at[1, z], sat_cells.at[1, z], sems.at[z, 2]),
+            ]
+        )
+        for copy in copies[-1]:
+            copy.start()
+
+    sources = (p_hbm, sat_hbm.at[0], sat_hbm.at[1], k_hbm)
+    first_plane = (1 - parity_s[0]) * (CZ - 1)
+    planes_in, sides_in = [], []
+    for f, source in enumerate(sources):
+        for kind, z in ((0, first_plane), (1, CZ - 1 - first_plane)):
+            planes_in.append(
+                pltpu.make_async_copy(source.at[z], planes.at[kind, f], plane_sems.at[kind, f])
+            )
+        for side, row in ((0, CX - 8), (1, 0)):
+            sides_in.append(
+                pltpu.make_async_copy(
+                    source.at[:, pl.ds(row, 8), :], edges.at[side, f], edge_sems.at[side, f]
+                )
+            )
+    for copy in planes_in + sides_in:
+        copy.start()
+
+    for copy in slots_in:
+        copy.wait()
     for half in range(2):
         cols = slice(half * LANES, (half + 1) * LANES)
         here = slice(half * OWNERS, (half + 1) * OWNERS)
-        cell = cell_ref[0, 0, :, cols]
-        seg = seg_ref[0, 0, :, cols]
+        cell = slots[0, :, cols]
+        seg = slots[2, :, cols]
         well = lax.shift_right_logical(seg, 1)
         group = lax.shift_right_logical(well * 2731, 16)
         rows_ref[here, :] = (
             (lax.shift_right_logical(cell, 7) & 1) * ROWS
-            + depth_ref[0, 0, :, cols] * CX
+            + slots[1, :, cols] * CX
             + lax.shift_right_logical(cell, 8)
         )
         ints_ref[0, here, :] = cell & (LANES - 1)
         ints_ref[1, here, :] = group
         ints_ref[2, here, :] = well - group * GROUP + (seg & 1) * HALF
-        floats_ref[0, here, :] = index_ref[0, 0, :, cols]
+        floats_ref[0, here, :] = index_slots[:, cols]
     to_smem.start()
 
-    def dense(i, carry):
-        z = lax.div(i, CX // 32)
-        row = pl.multiple_of((i - z * (CX // 32)) * 32, 32)
-        here = pl.ds(row, 32)
-        press = p_ref[z, here, :]
-        lam = mobilities(sat_ref[0, z, here, :], sat_ref[1, z, here, :])
-        total = lam[0] + lam[1] + lam[2]
-        for half in range(2):
-            at = pl.ds(pl.multiple_of(half * ROWS + 32 * i, 32), 32)
-            cols = slice(half * LANES, (half + 1) * LANES)
-            p_rows[at, :] = press[:, cols]
-            m_rows[at, :] = total[:, cols]
-        return carry
-
-    lax.fori_loop(0, CZ * CX // 32, dense, 0)
+    for z in range(CZ):
+        for copy in copies[z]:
+            copy.wait()
+
+        def dense(i, carry):
+            row = pl.multiple_of(32 * i, 32)
+            here = pl.ds(row, 32)
+            press = p_cells[z, here, :]
+            lam = mobilities(sat_cells[0, z, here, :], sat_cells[1, z, here, :])
+            total = lam[0] + lam[1] + lam[2]
+            for half in range(2):
+                at = pl.ds(pl.multiple_of(half * ROWS + z * CX + row, 32), 32)
+                cols = slice(half * LANES, (half + 1) * LANES)
+                p_rows[at, :] = press[:, cols]
+                m_rows[at, :] = total[:, cols]
+            return carry
+
+        lax.fori_loop(0, CX // 32, dense, 0)
+
     to_smem.wait()
     sub = iota((8, LANES), 0)
     lane = iota((8, LANES), 1)
@@ -104,7 +144,7 @@
     def pick(owner, carry):
         for half in range(2):
 
-            @pl.when(blocks_s[owner] > half)
+            @pl.when(blocks_s[0, 0, owner] > half)
             def _():
                 block = half * OWNERS + owner
                 for group in range(16):
@@ -123,10 +163,28 @@
 
     lax.fori_loop(0, OWNERS, pick, 0)
 
+    for copy in planes_in:
+        copy.wait()
+    planes_out = [
+        pltpu.make_async_copy(planes.at[0], plane_even_hbm, plane_sems.at[0, 0]),
+        pltpu.make_async_copy(planes.at[1], plane_odd_hbm, plane_sems.at[1, 0]),
+    ]
+    for copy in planes_out:
+        copy.start()
+    for copy in sides_in:
+        copy.wait()
+    swap = parity_s[1] == 1
+    for f in range(4):
+        for z in range(CZ):
+            last = edges[0, f, z, 7:8, :]
+            first = edges[1, f, z, 0:1, :]
+            row_even_ref[f, z : z + 1, :] = jnp.where(swap, first, last)
+            row_odd_ref[f, z : z + 1, :] = jnp.where(swap, last, first)
+
     def reduce(step, carry):
         for unit in range(UNROLL):
             owner = step * UNROLL + unit
-            count = blocks_s[owner]
+            count = blocks_s[0, 0, owner]
             values = []
             hots = []
             for half in range(2):
@@ -166,90 +224,53 @@
         return carry
 
     lax.fori_loop(0, OWNERS // UNROLL, reduce, 0)
-
-
-def gather_sums(blocks, pressure, saturations, cell, depth, seg, index):
+    for copy in planes_out:
+        copy.wait()
+
+
+def gather_sums(blocks, parity, pressure, saturations, permeability, cell, depth, seg, index):
+    smem = pl.BlockSpec(memory_space=pltpu.SMEM)
+    hbm = pl.BlockSpec(memory_space=pl.ANY)
     vmem = pl.BlockSpec(memory_space=pltpu.VMEM)
     return pl.pallas_call(
         gather_kernel,
-        in_specs=[pl.BlockSpec(memory_space=pltpu.SMEM)] + [vmem] * 6,
-        out_specs=[vmem] * 4,
+        in_specs=[smem, smem] + [hbm] * 7,
+        out_specs=[vmem] * 4 + [hbm] * 2 + [vmem] * 2,
         out_shape=[
             jax.ShapeDtypeStruct((DEVICES, LANES), F32),
             jax.ShapeDtypeStruct((2 * OWNERS, LANES), I32),
             jax.ShapeDtypeStruct((3, 2 * OWNERS, LANES), I32),
             jax.ShapeDtypeStruct((2, 2 * OWNERS, LANES), F32),
+            pltpu.HBM((4, CX, CY), F32),
+            pltpu.HBM((4, CX, CY), F32),
+            jax.ShapeDtypeStruct((4, CZ, CY), F32),
+            jax.ShapeDtypeStruct((4, CZ, CY), F32),
         ],
         scratch_shapes=[
+            pltpu.VMEM((CZ, CX, CY), F32),
+            pltpu.VMEM((2, CZ, CX, CY), F32),
             pltpu.VMEM((2 * ROWS, LANES), F32),
             pltpu.VMEM((2 * ROWS, LANES), F32),
             pltpu.VMEM((2 * OWNERS, LANES, LANES), F32),
             pltpu.VMEM((2 * OWNERS, LANES, LANES), F32),
             pltpu.SMEM((2 * OWNERS, LANES), I32),
+            pltpu.VMEM((2, 4, CZ, 8, CY), F32),
+            pltpu.VMEM((2, 4, CX, CY), F32),
+            pltpu.VMEM((3, OWNERS, SLOTS), I32),
+            pltpu.VMEM((OWNERS, SLOTS), F32),
             pltpu.SemaphoreType.DMA(()),
+            pltpu.SemaphoreType.DMA((CZ, 3)),
+            pltpu.SemaphoreType.DMA((2, 4)),
+            pltpu.SemaphoreType.DMA((2, 4)),
+            pltpu.SemaphoreType.DMA((4,)),
         ],
-        compiler_params=pltpu.CompilerParams(vmem_limit_bytes=10 << 20),
+        compiler_params=pltpu.CompilerParams(vmem_limit_bytes=24 << 20),
         cost_estimate=pl.CostEstimate(flops=0, bytes_accessed=24 << 20, transcendentals=0),
         name="gather_sums",
-    )(blocks, in_vmem(pressure), in_vmem(saturations), cell, depth, seg, index)
-
-
-def pack_kernel(
-    parity_s, p_hbm, sat_hbm, k_hbm, plane_even_ref, plane_odd_ref, row_even_ref, row_odd_ref, edges, sems
-):
-    z_odd, x_odd = parity_s[0], parity_s[1]
-    sources = (p_hbm, sat_hbm.at[0], sat_hbm.at[1], k_hbm)
-    planes, sides = [], []
-    for f, source in enumerate(sources):
-        first = (1 - z_odd) * (CZ - 1)
-        planes.append(
-            pltpu.make_async_copy(source.at[first], plane_even_ref.at[f], sems.at[0, f])
-        )
-        planes.append(
-            pltpu.make_async_copy(source.at[CZ - 1 - first], plane_odd_ref.at[f], sems.at[1, f])
-        )
-        for side, row in ((0, CX - 8), (1, 0)):
-            sides.append(
-                pltpu.make_async_copy(
-                    source.at[:, pl.ds(row, 8), :], edges.at[side, f], sems.at[2 + side, f]
-                )
-            )
-    for copy in sides + planes:
-        copy.start()
-    for copy in sides:
-        copy.wait()
-    swap = x_odd == 1
-    for f in range(4):
-        for z in range(CZ):
-            last = edges[0, f, z, 7:8, :]
-            first = edges[1, f, z, 0:1, :]
-            row_even_ref[f, z : z + 1, :] = jnp.where(swap, first, last)
-            row_odd_ref[f, z : z + 1, :] = jnp.where(swap, last, first)
-    for copy in planes:
-        copy.wait()
-
-
-def pack_halos(parity, pressure, saturations, permeability):
-    hbm = pl.BlockSpec(memory_space=pl.ANY)
-    vmem = pl.BlockSpec(memory_space=pltpu.VMEM)
-    return pl.pallas_call(
-        pack_kernel,
-        in_specs=[pl.BlockSpec(memory_space=pltpu.SMEM)] + [hbm] * 3,
-        out_specs=[vmem] * 4,
-        out_shape=[
-            pltpu.VMEM((4, CX, CY), F32),
-            pltpu.VMEM((4, CX, CY), F32),
-            jax.ShapeDtypeStruct((4, CZ, CY), F32),
-            jax.ShapeDtypeStruct((4, CZ, CY), F32),
-        ],
-        scratch_shapes=[
-            pltpu.VMEM((2, 4, CZ, 8, CY), F32),
-            pltpu.SemaphoreType.DMA((4, 4)),
-        ],
-        compiler_params=pltpu.CompilerParams(vmem_limit_bytes=4 << 20),
-        cost_estimate=pl.CostEstimate(flops=0, bytes_accessed=6 << 20, transcendentals=0),
-        name="pack_halos",
-    )(parity, in_hbm(pressure), in_hbm(saturations), in_hbm(permeability))
+    )(
+        in_hbm(blocks), parity,
+        *[in_hbm(v) for v in (pressure, saturations, permeability, cell, depth, seg, index)],
+    )
 
 
 def solve_kernel(sums_ref, parent_ref, cond_ref, target_ref, send_ref, parts):
@@ -671,9 +692,9 @@
     def exchange(values):
         return lax.all_to_all(values, ("areal", "layer"), split_axis=0, concat_axis=0, tiled=True)
 
-    packed = pack_halos(parity, pressure, saturations, permeability)
-    sums, rows, ints, floats = gather_sums(
-        blocks, pressure, saturations, perf_cell, perf_layer, perf_seg, perf_index
+    sums, rows, ints, floats, *packed = gather_sums(
+        perf_blocks, parity, pressure, saturations, permeability,
+        perf_cell, perf_layer, perf_seg, perf_index,
     )
     received = exchange(sums)
     plane_even = even_swap(packed[0], "layer", n_layer)

time: 77.2 us -> 77.3 us (level)
  starting transfers between devices: 24.9 us -> 25.9 us
  Pallas kernels: 39.1 us -> 38.3 us
    all_to_all x2, starting transfers between devices: 17.7 us -> 19.5 us  [exchange(): lax.all_to_all(values, ('areal', 'layer'), split_axis=0, concat_axis=0, t...]
    ppermute x2, starting transfers between devices: 5.62 us -> 4.83 us  [odd_swap(): return lax.ppermute(values, axis, pairs + [(j, i) for i, j in pairs])]
    pallas_call x2 -> x1, Pallas kernels: 11.6 us -> 11.2 us  [gather_sums(): pl.pallas_call(gather_kernel, in_specs=[smem, smem] + [hbm] * 7, out_spec...]
  transfers between devices with their start and end apart: 6 -> 6, of which waited for: 2 -> 2; matrix products, arithmetic and copies ran while one was open for 0% -> 0% of each run, Pallas kernels for 32% -> 21%
where the time goes in v2:
time: 77.3 us; the launch traced here: 76.9 us
  Pallas kernels  38.3 us (50%)
  starting transfers between devices  25.9 us (34%)
  waiting for transfers between devices  11.7 us (15%)
    all_to_all x2, starting transfers between devices, exchange(): lax.all_to_all(values, ('areal', 'layer'), split_axis=0, concat_axis=0, t...  19.5 us
    pallas_call x1, Pallas kernels, cell_flows(): pl.pallas_call(flow_kernel, grid=(CZ,), in_specs=[pl.BlockSpec(memory_spa...  15.5 us
    pallas_call x1, Pallas kernels, gather_sums(): pl.pallas_call(gather_kernel, in_specs=[smem, smem] + [hbm] * 7, out_spec...  11.2 us
    pallas_call x1, Pallas kernels, add_inflow(): pl.pallas_call(inflow_kernel, grid_spec=pltpu.PrefetchScalarGridSpec(num_...  10.6 us
    all_to_all x2, waiting for transfers between devices, exchange(): lax.all_to_all(values, ('areal', 'layer'), split_axis=0, concat_axis=0, t...  7.77 us
    ppermute x2, starting transfers between devices, odd_swap(): return lax.ppermute(values, axis, pairs + [(j, i) for i, j in pairs])  4.83 us
    ppermute x2, waiting for transfers between devices, odd_swap(): return lax.ppermute(values, axis, pairs + [(j, i) for i, j in pairs])  3.92 us
    ppermute x2, starting transfers between devices, even_swap(): return lax.ppermute(values, axis, [(i, i ^ 1) for i in range(count)])  1.63 us
  transfers between devices with their start and end apart: 6, of which 2 were waited for; matrix products, arithmetic and copies ran while one was open for 0% of the time, Pallas kernels for 21%

profile of v2, /device:TPU:4, one launch (start us, length us, event | category | flops | bytes accessed | tf_op | source)
XLA Modules:
  0.0 76.9 jit_solution(370342315524740604)
XLA Ops:
  0.6 0.0 copy-start
  0.6 0.1 add_and_fusion.parity_s
  0.7 11.2 %gather_sums.1 = (f32[128,128]{1,0:T(8,128)}, s32[32,128]{1,0:T(8,128)S(1)}, s32[3,32,128]{2,1,0:T(8,128)S(1)}, f32[2,32,128]{2,1,0:T(8,128)S(1)}, f32[4,256,256...) custom-call(s32[1,1,16]{2,1,0:T(1,128)} %blocks_s.1, ...), custom_call_target="tpu_custom_call" | custom-call | bytes 25165824 | tf_op jit(solution)/shard_map/gather_sums/pallas_call | solution.py:235
  11.9 0.1 collective-permute-start
  12.0 0.7 collective-permute-start.1
  12.7 12.7 %all-to-all-start = ((f32[128,1,128]{2,1,0:T(1,128)}), f32[128,1,128]{2,1,0:T(1,128)S(1)}, u32[]{:S(2)}, u32[]{:S(2)}) async-start(f32[128,1,128]{2,1,0:T(1,128)} %bitcast.4), calls=%async_computation | async-start | bytes 131072 | tf_op jit(solution)/shard_map/all_to_all | solution.py:693
  25.5 0.0 copy-done
  25.5 0.1 dynamic-slice_bitcast_fusion.2
  25.6 0.0 copy-done.2
  25.6 0.0 copy-done.3
  25.6 0.1 dynamic-slice_bitcast_fusion
  25.7 7.8 %all-to-all-done = f32[128,1,128]{2,1,0:T(1,128)S(1)} async-done(((f32[128,1,128]{2,1,0:T(1,128)}), f32[128,1,128]{2,1,0:T(1,128)S(1)}, u32[]{:S(2)}, u32[]{:S(2)}) %all-to-all-start) | async-done | bytes 65568 | tf_op jit(solution)/shard_map/all_to_all | solution.py:693
  33.4 1.0 %solve_wells.1 = f32[128,128]{1,0:T(8,128)} custom-call(f32[128,128]{1,0:T(8,128)S(1)} %bitcast.19, s32[16,128]{1,0:T(8,128)S(1)} %pad.11.parent_ref, f32[16,128]{1,0:T(8,128)S(1)} %pad.12.cond_ref, f32[16,128]{1,0:T(8,128)S(1)} %pad.13.target_ref), custom_call_target="tpu_custom_call" | custom-call | bytes 1048576 | tf_op jit(solution)/shard_map/solve_wells/pallas_call | solution.py:318
  34.5 6.7 %all-to-all-start.1 = ((f32[128,1,128]{2,1,0:T(1,128)}), f32[128,1,128]{2,1,0:T(1,128)S(1)}, u32[]{:S(2)}, u32[]{:S(2)}) async-start(f32[128,1,128]{2,1,0:T(1,128)} %bitcast.10), calls=%async_computation.1 | async-start | bytes 131072 | tf_op jit(solution)/shard_map/all_to_all | solution.py:693
  41.2 1.5 %collective-permute-start.2 = (f32[4,8,256]{2,1,0:T(8,128)S(1)}, f32[4,8,256]{2,1,0:T(8,128)S(1)}, u32[]{:S(2)}, u32[]{:S(2)}) collective-permute-start(f32[4,8,256]{2,1,0:T(8,128)S(1)} %get-tuple-element.18), channel_id=1, source_target_pairs={{0,8},{8,0},{16,24},{24,16},{32,40},{40,32},{48,56},{56,48},{64,72... | collective-permute-start | bytes 98312 | tf_op jit(solution)/shard_map/ppermute | solution.py:686
  42.7 4.1 %collective-permute-start.3 = (f32[4,8,256]{2,1,0:T(8,128)S(1)}, f32[4,8,256]{2,1,0:T(8,128)S(1)}, u32[]{:S(2)}, u32[]{:S(2)}) collective-permute-start(f32[4,8,256]{2,1,0:T(8,128)S(1)} %get-tuple-element.19), channel_id=1, source_target_pairs={{8,16},{24,32},{40,48},{56,64},{72,80},{88,96},{104,112},{16,8},{3... | collective-permute-start | bytes 98312 | tf_op jit(solution)/shard_map/ppermute | solution.py:690
  46.9 0.0 collective-permute-done.2.row_even_ref
  46.9 3.9 %collective-permute-done.3.row_odd_ref = f32[4,8,256]{2,1,0:T(8,128)S(1)} collective-permute-done((f32[4,8,256]{2,1,0:T(8,128)S(1)}, f32[4,8,256]{2,1,0:T(8,128)S(1)}, u32[]{:S(2)}, u32[]{:S(2)}) %collective-permute-start.3) | collective-permute-done | bytes 32800 | tf_op jit(solution)/shard_map/ppermute | solution.py:690
  50.8 0.0 collective-permute-done.plane_even_ref
  50.8 0.0 collective-permute-done.1.plane_odd_ref
  50.8 15.5 %cell_flows.1.flow_hbm = f32[3,8,256,256]{3,2,1,0:T(8,128)} custom-call(s32[2]{0:T(128)S(1)} %add_and_fusion.parity_s, f32[8,256,256]{2,1,0:T(8,128)} %p_hbm.3, f32[2,8,256,256]{3,2,1,0:T(8,128)} %sat_hbm.5, f32[8,256,256]{2,1,0:T(8,128)} %k_hbm.3, f32[4,256,256]{2,1,0:T(8,128)S(1)} %collective-permute-done.plane_even_ref, ...), custom_call_target="tpu_custom_call" | custom-call | bytes 20971520 | tf_op jit(solution)/shard_map/cell_flows/pallas_call | solution.py:507
  66.3 0.0 all-to-all-done.1
  66.3 0.0 copy-done.1
  66.3 10.6 %add_inflow.1 = (f32[3,8,256,256]{3,2,1,0:T(8,128)}, f32[2,192]{1,0:T(2,128)}) custom-call(s32[32,128]{1,0:T(8,128)S(1)} %get-tuple-element.12.rows_s, s32[16]{0:T(128)S(1)} %bitcast.20, s32[1]{0:T(128)} %bitcast.1.areal_s, f32[128,128]{1,0:T(8,128)S(1)} %bitcast.18, s32[3,32,128]{2,1,0:T(8,128)S(1)} %get-tuple-element.14.ints_ref, ...), custom_call_target="tpu_custom_call" | custom-call | bytes 25165824 | tf_op jit(solution)/shard_map/add_inflow/pallas_call | solution.py:628
  (6 shorter events, 0.0 us)
Async XLA Ops:
  0.6 24.8 %copy-start = (s32[192,16]{0,1:T(8,128)S(1)}, s32[192,16]{0,1:T(8,128)}, u32[]{:S(2)}) copy-start(s32[192,16]{0,1:T(8,128)} %param.23) | copy-start | bytes 36868
  0.7 24.8 %copy-start.2 = (f32[192,16]{0,1:T(8,128)S(1)}, f32[192,16]{0,1:T(8,128)}, u32[]{:S(2)}) copy-start(f32[192,16]{0,1:T(8,128)} %param.25) | copy-start | bytes 36868
  0.7 24.8 %copy-start.3 = (f32[192,16]{0,1:T(8,128)S(1)}, f32[192,16]{0,1:T(8,128)}, u32[]{:S(2)}) copy-start(f32[192,16]{0,1:T(8,128)} %param.24) | copy-start | bytes 36868
  11.9 38.9 %collective-permute-start = (f32[4,256,256]{2,1,0:T(8,128)}, f32[4,256,256]{2,1,0:T(8,128)S(1)}, u32[]{:S(2)}, u32[]{:S(2)}) collective-permute-start(f32[4,256,256]{2,1,0:T(8,128)} %get-tuple-element.16), channel_id=1, source_target_pairs={{0,1},{1,0},{2,3},{3,2},{4,5},{5,4},{6,7},{7,6},{8,9},{9,8},{10,11... | collective-permute-start | bytes 3145736 | tf_op jit(solution)/shard_map/ppermute | solution.py:686
  12.0 38.8 %collective-permute-start.1 = (f32[4,256,256]{2,1,0:T(8,128)}, f32[4,256,256]{2,1,0:T(8,128)S(1)}, u32[]{:S(2)}, u32[]{:S(2)}) collective-permute-start(f32[4,256,256]{2,1,0:T(8,128)} %get-tuple-element.17), channel_id=1, source_target_pairs={{1,2},{3,4},{5,6},{2,1},{4,3},{6,5},{9,10},{11,12},{13,14},{10,9},... | collective-permute-start | bytes 3145736 | tf_op jit(solution)/shard_map/ppermute | solution.py:690
  12.7 20.7 %all-to-all-start = ((f32[128,1,128]{2,1,0:T(1,128)}), f32[128,1,128]{2,1,0:T(1,128)S(1)}, u32[]{:S(2)}, u32[]{:S(2)}) async-start(f32[128,1,128]{2,1,0:T(1,128)} %bitcast.4), calls=%async_computation | async-start | bytes 131072 | tf_op jit(solution)/shard_map/all_to_all | solution.py:693
  34.5 31.8 %all-to-all-start.1 = ((f32[128,1,128]{2,1,0:T(1,128)}), f32[128,1,128]{2,1,0:T(1,128)S(1)}, u32[]{:S(2)}, u32[]{:S(2)}) async-start(f32[128,1,128]{2,1,0:T(1,128)} %bitcast.10), calls=%async_computation.1 | async-start | bytes 131072 | tf_op jit(solution)/shard_map/all_to_all | solution.py:693
  41.2 5.7 %collective-permute-start.2 = (f32[4,8,256]{2,1,0:T(8,128)S(1)}, f32[4,8,256]{2,1,0:T(8,128)S(1)}, u32[]{:S(2)}, u32[]{:S(2)}) collective-permute-start(f32[4,8,256]{2,1,0:T(8,128)S(1)} %get-tuple-element.18), channel_id=1, source_target_pairs={{0,8},{8,0},{16,24},{24,16},{32,40},{40,32},{48,56},{56,48},{64,72... | collective-permute-start | bytes 98312 | tf_op jit(solution)/shard_map/ppermute | solution.py:686
  42.7 23.5 %copy-start.1 = (s32[1,1,16]{2,1,0:T(1,128)S(1)}, s32[1,1,16]{2,1,0:T(1,128)}, u32[]{:S(2)}) copy-start(s32[1,1,16]{2,1,0:T(1,128)} %blocks_s.1) | copy-start | bytes 196
  42.7 8.0 %collective-permute-start.3 = (f32[4,8,256]{2,1,0:T(8,128)S(1)}, f32[4,8,256]{2,1,0:T(8,128)S(1)}, u32[]{:S(2)}, u32[]{:S(2)}) collective-permute-start(f32[4,8,256]{2,1,0:T(8,128)S(1)} %get-tuple-element.19), channel_id=1, source_target_pairs={{8,16},{24,32},{40,48},{56,64},{72,80},{88,96},{104,112},{16,8},{3... | collective-permute-start | bytes 98312 | tf_op jit(solution)/shard_map/ppermute | solution.py:690
